TPU v7x, 32 devices: a whole 2x2x4 slice. The times are simulated.
32 devices in a mesh: rows: 8 (over z, x), feat: 4 (over y, core).
Axes of the slice: x: 2, y: 2, z: 4, core: 2. Of those that a mesh axis runs over, the one named last changes fastest.
Arguments:
- features: float32 [16384, 1024], P('rows', 'feat')
- norm_gain: float32 [1024], P('feat'), may hold values from 0.1 to 1.9
- row_counts: int32 [8, 16], P('rows'), may hold values from 1 to 43, 86 in all within a row
- tile_cols: int32 [688], P('rows'), may hold values from 0 to 127, as said below
- tile_values: float32 [688, 128, 128], P('rows'), may hold values from -0.1875 to 0.1875
Outputs:
- normed: float32 [16384, 1024], P('rows', 'feat')
Inputs may be any that keep to these rules, and one draw needn't show every extreme that they name: `tile_cols`: node n lies in stripe n // 2048. There are exactly 3 heavy stripes; every device's tiles reference every block of every heavy stripe and every block of its own stripe. Every other block that a device's tiles reference is referenced by one of its tiles only, lies in no heavy stripe, and no two such blocks of one device lie in the same stripe; each device has exactly 3 such blocks. `row_counts`: each device's counts sum to 86.
All inputs are finite; a program needn't handle non-finite values.
Results may differ from a plain program's by a relative error of at most 0.0003.
Values sent between devices are 32-bit elements; how exact they have to be, the bound alone decides.
No kernel may reach another device: no remote copies, remote signals or barrier semaphores. Data moves between devices by JAX's collectives and lax.ppermute only.
A program may use at most 128 MiB of HBM per device.

v0:
```python
import jax
import jax.numpy as jnp
from jax import lax
from jax.sharding import PartitionSpec as P

HEAVY = 3


def broadcast(block, axis, owner):
    block = jnp.where(lax.axis_index(axis) == owner, block, jnp.zeros_like(block))
    return lax.psum(block, axis)


def per_device(features, norm_gain, row_counts, tile_cols, tile_values):
    node_dev, feat_dev = features.shape
    block_rows = tile_values.shape[1]
    blocks_dev = node_dev // block_rows
    tile_total = tile_values.shape[0]
    heavy_count = HEAVY
    devices = lax.axis_size("rows")
    my_index = lax.axis_index("rows")
    activated = jnp.maximum(features, 0.0)
    act_blocks = activated.reshape(blocks_dev, block_rows, feat_dev)
    owner_dev = tile_cols // blocks_dev
    local_block = tile_cols % blocks_dev
    is_own = owner_dev == my_index
    peer_ids = jnp.arange(devices, dtype=jnp.int32)
    block_ids = jnp.arange(blocks_dev, dtype=jnp.int32)
    to_peer = (owner_dev[None, :] == peer_ids[:, None]) & jnp.logical_not(is_own)[None, :]
    block_hit = jnp.any(
        to_peer[:, None, :] & (local_block[None, None, :] == block_ids[None, :, None]), axis=2
    )
    seen_count = jnp.sum(block_hit.astype(jnp.int32), axis=1)
    local_mark = (seen_count >= 2).astype(jnp.int32)
    heavy_mark = lax.pmax(local_mark, "rows")
    heavy_rank = jnp.cumsum(heavy_mark, dtype=jnp.int32) - 1
    heavy_list = []
    for stripe in range(heavy_count):
        heavy_list.append(
            jnp.sum(jnp.where((heavy_mark > 0) & (heavy_rank == stripe), peer_ids, 0))
        )
    heavy_ids = jnp.stack(heavy_list)
    stripes = []
    for stripe in range(heavy_count):
        stripes.append(broadcast(activated, "rows", heavy_ids[stripe]))
    heavy_blocks = jnp.stack(stripes).reshape(heavy_count * blocks_dev, block_rows, feat_dev)
    match_heavy = owner_dev[:, None] == heavy_ids[None, :]
    is_heavy = jnp.any(match_heavy, axis=1) & jnp.logical_not(is_own)
    stripe_ids = jnp.arange(heavy_count, dtype=jnp.int32)
    heavy_slot = (
        jnp.sum(match_heavy.astype(jnp.int32) * stripe_ids[None, :], axis=1) * blocks_dev
        + local_block
    )
    is_light = jnp.logical_not(is_own | is_heavy)
    to_owner = is_light[None, :] & (owner_dev[None, :] == peer_ids[:, None])
    wanted = jnp.max(jnp.where(to_owner, local_block[None, :], -1), axis=1)
    requested = lax.all_to_all(
        wanted.reshape(devices, 1), "rows", split_axis=0, concat_axis=0, tiled=True
    )[:, 0]
    request_valid = requested >= 0
    served = act_blocks[jnp.maximum(requested, 0)]
    outgoing = jnp.where(request_valid[:, None, None], served, 0.0)
    tile_counts = row_counts[0]
    row_ends = jnp.cumsum(tile_counts, dtype=jnp.int32)
    tile_index = jnp.arange(tile_total, dtype=jnp.int32)
    tile_row = jnp.sum((row_ends[None, :] <= tile_index[:, None]).astype(jnp.int32), axis=1)
    row_ids = jnp.arange(blocks_dev, dtype=jnp.int32)
    tile_of_owner = jnp.max(jnp.where(to_owner, tile_index[None, :], -1), axis=1)
    has_light = tile_of_owner >= 0
    light_tile = jnp.maximum(tile_of_owner, 0)
    light_values = jnp.where(has_light[:, None, None], tile_values[light_tile], 0.0)
    light_row = tile_row[light_tile]
    light_onehot = ((light_row[None, :] == row_ids[:, None]) & has_light[None, :]).astype(
        jnp.float32
    )
    piece = lax.all_to_all(outgoing, "rows", split_axis=0, concat_axis=0, tiled=True)
    width = piece.shape[2]
    partial_value = jnp.einsum("nij,njf->nif", light_values, piece, precision=lax.Precision.HIGHEST)
    summed = jnp.dot(
        light_onehot,
        partial_value.reshape(devices, block_rows * width),
        precision=lax.Precision.HIGHEST,
        preferred_element_type=jnp.float32,
    )
    light_sum = summed.reshape(node_dev, width)
    light_need = (devices - heavy_count - 1) * 3 // 4
    near_count = tile_total - light_need
    ranking = jnp.argsort(is_light.astype(jnp.int32), stable=True)[:near_count]
    near_panel = jnp.concatenate([heavy_blocks, act_blocks], axis=0)
    near_slot = jnp.where(is_own, heavy_count * blocks_dev + local_block, heavy_slot)[ranking]
    picked = near_panel[near_slot]
    products = jnp.einsum(
        "tij,tjf->tif", tile_values[ranking], picked, precision=lax.Precision.HIGHEST
    )
    near_onehot = (tile_row[ranking][None, :] == row_ids[:, None]).astype(jnp.float32)
    near_sum = jnp.dot(
        near_onehot,
        products.reshape(near_count, block_rows * feat_dev),
        precision=lax.Precision.HIGHEST,
        preferred_element_type=jnp.float32,
    )
    aggregate = near_sum.reshape(node_dev, feat_dev) + light_sum
    square_sum = lax.psum(jnp.sum(aggregate * aggregate, axis=1), "feat")
    mean_square = square_sum / (feat_dev * lax.axis_size("feat"))
    return aggregate * norm_gain[None, :] * lax.rsqrt(mean_square + 1e-05)[:, None]


def solution(mesh):
    placed = (P("rows", "feat"), P("feat"), P("rows", None), P("rows"), P("rows", None, None))
    return jax.shard_map(
        per_device, mesh=mesh, in_specs=placed, out_specs=P("rows", "feat"), check_vma=False
    )
```

profile of v0, /device:TPU:0, one launch (start us, length us, event | category | flops | bytes accessed | tf_op | source)
XLA Modules:
  0.0 341.9 jit_solution(11381033158909850786)
XLA Ops:
  8.2 13.1 %pmax.7 = s32[8]{0:T(128)S(1)} all-reduce(s32[8]{0:T(128)S(1)} %compare_convert_fusion), channel_id=1, replica_groups=mesh['rows'=8,'feat'=4] {'rows'}, use_global_device_ids=true, to_apply=%region_4.5 | all-reduce | flops 8 | bytes 64 | tf_op jit(solution)/shard_map/pmax | solution.py:35
  24.2 4.6 %select_bitcast_fusion.2 = (f32[1,2048,256]{2,1,0:T(8,128)}, f32[1,2048,256]{2,1,0:T(8,128)}, f32[1,2048,256]{2,1,0:T(8,128)}, f32[2048,256]{1,0:T(8,128)S(1)}) fusion(pred[]{:T(512)S(6)} %eq.136, f32[2048,256]{1,0:T(8,128)} %param.5, pred[]{:T(512)S(6)} %eq.137, pred[]{:T(512)S(6)} %eq.138), kind=kLoop, calls=%fused_computation.14 | loop fusion | flops 2097152 | bytes 10485763 | tf_op jit(solution)/shard_map/stack | solution.py:46
  28.8 2.0 pad_add_fusion
  31.1 9.3 %all_to_all.14 = s32[8,1,1]{2,1,0:T(1,128)S(1)} all-to-all(s32[8,1,1]{2,1,0:T(1,128)S(1)} %copy.13), channel_id=1, replica_groups=mesh['rows'=8,'feat'=4] {'rows'}, dimensions={0} | all-to-all | bytes 64 | tf_op jit(solution)/shard_map/all_to_all | solution.py:57
  42.7 3.6 %all-to-all-start.1 = ((f32[8,128,256]{2,1,0:T(8,128)}), f32[8,128,256]{2,1,0:T(8,128)S(1)}, u32[]{:S(2)}, u32[]{:S(2)}) async-start(f32[8,128,256]{2,1,0:T(8,128)} %broadcast_select_fusion), calls=%async_computation.1 | async-start | bytes 2097152 | tf_op jit(solution)/shard_map/all_to_all | solution.py:76
  46.5 2.6 sort.17
  49.9 1.2 gather_fusion
  51.1 4.0 %gather_fusion.5 = f32[8,128,128]{2,1,0:T(8,128)} fusion(f32[86,128,128]{2,1,0:T(8,128)} %param.9, s32[1024]{0:T(1024)S(1)} %pad_clamp_fusion.1), kind=kCustom, calls=%fused_computation.5 | custom fusion | bytes 1048608 | tf_op jit(solution)/shard_map/gather | solution.py:71
  55.1 5.9 %gather_fusion.1 = f32[83,128,128]{2,1,0:T(8,128)} fusion(f32[86,128,128]{2,1,0:T(8,128)} %param.9, s32[1024]{0:T(1024)S(1)} %pad_clamp_fusion.3), kind=kCustom, calls=%fused_computation.1 | custom fusion | bytes 10879308 | tf_op jit(solution)/shard_map/gather | solution.py:93
  62.4 35.4 %all-to-all-done.1 = f32[8,128,256]{2,1,0:T(8,128)S(1)} async-done(((f32[8,128,256]{2,1,0:T(8,128)}), f32[8,128,256]{2,1,0:T(8,128)S(1)}, u32[]{:S(2)}, u32[]{:S(2)}) %all-to-all-start.1) | async-done | bytes 1048608 | tf_op jit(solution)/shard_map/all_to_all | solution.py:76
  97.8 2.1 convolution_bitcast_fusion
  99.9 1.7 copy.15
  101.6 158.5 %all-reduce.3.cloned.1.call-done = (f32[1,2048,256]{2,1,0:T(8,128)}, f32[1,2048,256]{2,1,0:T(8,128)}, f32[1,2048,256]{2,1,0:T(8,128)}) async-done(((f32[1,2048,256]{2,1,0:T(8,128)}, f32[1,2048,256]{2,1,0:T(8,128)}, f32[1,2048,256]{2,1,0:T(8,128)}), (f32[1,2048,256]{2,1,0:T(8,128)}, f32[1,2048,256]{2,1,0:T(8,128)}, f32[1,2048,256]{2,1,0:T(8,128)})) %all-reduce.3.cloned.1.call-update) | async-done | bytes 6291472 | tf_op jit(solution)/shard_map/psum | solution.py:11
  260.0 3.3 pad_maximum_fusion.1
  263.3 3.9 %pad_maximum_fusion = f32[64,128,256]{2,1,0:T(8,128)} fusion(f32[16,128,256]{2,1,0:T(8,128)S(1)} %bitcast.51, f32[48,128,256]{2,1,0:T(8,128)S(1)} %bitcast.49), kind=kLoop, calls=%fused_computation.8 | loop fusion | flops 2097152 | bytes 16777216 | tf_op jit(solution)/shard_map/concatenate | solution.py:89
  267.2 11.7 %gather_fusion.3 = f32[83,128,256]{2,1,0:T(8,128)} fusion(f32[64,128,256]{2,1,0:T(8,128)} %pad_maximum_fusion, s32[1024]{0:T(1024)S(1)} %pad_clamp_fusion.2), kind=kCustom, calls=%fused_computation.3 | custom fusion | bytes 21758284 | tf_op jit(solution)/shard_map/gather | solution.py:91
  278.8 15.2 %fusion.22 = f32[83,128,256]{2,1,0:T(8,128)S(1)} fusion(f32[83,128,128]{2,1,0:T(8,128)} %gather_fusion.1, f32[83,128,256]{2,1,0:T(8,128)} %gather_fusion.3), kind=kOutput, calls=%fused_computation.77 | convolution fusion | flops 4177526784 | bytes 27197440 | tf_op jit(solution)/shard_map/tij,tjf->tif/dot_general | solution.py:92
  294.0 5.5 %pad.15 = f32[88,128,256]{2,1,0:T(8,128)} pad(f32[83,128,256]{2,1,0:T(8,128)S(1)} %fusion.22, f32[]{:T(128)} %constant.66.clone.1), padding=0_5x0_0x0_0 | pad | bytes 22413316
  299.5 16.1 %copy.14 = f32[11,8,128,256]{3,1,2,0:T(8,128)} copy(f32[11,8,128,256]{3,2,1,0:T(8,128)} %bitcast.47) | data formatting | bytes 23068672
  315.7 6.9 %fusion.3 = f32[16,32768]{1,0:T(8,128)S(1)} fusion(f32[83,32768]{1,0:T(8,128)} %bitcast.48, s32[83]{0:T(128)S(1)} %gather_fusion), kind=kOutput, calls=%fused_computation.29 | convolution fusion | flops 522192192 | bytes 12976460 | tf_op jit(solution)/shard_map/dot_general | solution.py:96
  322.6 2.4 convolution_add_fusion
  325.0 1.7 add.67
  327.1 6.4 %psum.31 = f32[2048]{0:T(1024)S(1)} all-reduce(f32[2048]{0:T(1024)S(1)} %multiply_reduce_fusion), channel_id=1, replica_groups=mesh['rows'=8,'feat'=4] {'feat'}, use_global_device_ids=true, to_apply=%region_18.19 | all-reduce | flops 2048 | bytes 16384 | tf_op jit(solution)/shard_map/psum | solution.py:103
  333.4 1.7 multiply_multiply_fusion
  (46 shorter events, 7.9 us)
Async XLA Ops:
  6.5 253.5 %all-reduce.3.cloned.1.call-start = ((), (), s32[]{:S(2)}) async-start(), calls=%async_computation.2 | async-start | bytes 12582912 | tf_op jit(solution)/shard_map/psum | solution.py:11
  28.8 17.5 %copy-start.3 = (s32[1,16]{1,0:T(1,128)S(1)}, s32[1,16]{1,0:T(1,128)}, u32[]{:S(2)}) copy-start(s32[1,16]{1,0:T(1,128)} %param.7) | copy-start | bytes 196
  42.7 55.0 %all-to-all-start.1 = ((f32[8,128,256]{2,1,0:T(8,128)}), f32[8,128,256]{2,1,0:T(8,128)S(1)}, u32[]{:S(2)}, u32[]{:S(2)}) async-start(f32[8,128,256]{2,1,0:T(8,128)} %broadcast_select_fusion), calls=%async_computation.1 | async-start | bytes 2097152 | tf_op jit(solution)/shard_map/all_to_all | solution.py:76
  55.1 6.0 %copy-start.1 = (s32[86]{0:T(128)S(1)}, s32[86]{0:T(128)}, u32[]{:S(2)}) copy-start(s32[86]{0:T(128)} %param.8) | copy-start | bytes 1036
  315.7 6.9 %copy-start = (f32[1,8,128,256]{3,1,2,0:T(8,128)S(1)}, f32[1,8,128,256]{3,1,2,0:T(8,128)}, u32[]{:S(2)}) copy-start(f32[1,8,128,256]{3,1,2,0:T(8,128)} %copy.15) | copy-start | bytes 3145732
  322.6 10.8 %copy-start.2 = (f32[256]{0:T(256)S(1)}, f32[256]{0:T(256)}, u32[]{:S(2)}) copy-start(f32[256]{0:T(256)} %param.6) | copy-start | bytes 3076
Sparse Core Ops, SparseCore 0:
  29.0 231.0 all-reduce.2
where the time goes:
time: 342 us
  waiting for transfers between devices  194 us (57%)
  local copies, waits for them, and re-layouts  50.5 us (15%)
  blocking collectives  28.8 us (8%)
  matrix products  26.6 us (8%)
  other arithmetic  23.2 us (7%)
  between operations  15.5 us (5%)
  starting transfers between devices  3.56 us (1%)
    psum x1, waiting for transfers between devices, broadcast(): return lax.psum(block, axis)  158 us
    all_to_all x1, waiting for transfers between devices, per_device(): lax.all_to_all(outgoing, 'rows', split_axis=0, concat_axis=0, tiled=True)  35.4 us
    unnamed x11, local copies, waits for them, and re-layouts  23.3 us
    dot_general x1, matrix products, per_device(): jnp.einsum('tij,tjf->tif', tile_values[ranking], picked, precision=lax.Pr...  15.2 us
    pmax x1, blocking collectives, per_device(): heavy_mark = lax.pmax(local_mark, 'rows')  13.1 us
    gather x1, local copies, waits for them, and re-layouts, per_device(): picked = near_panel[near_slot]  11.7 us
    all_to_all x1, blocking collectives, per_device(): lax.all_to_all(wanted.reshape(devices, 1), 'rows', split_axis=0, concat_a...  9.31 us
    another operation x2, other arithmetic, per_device(): jnp.stack(stripes).reshape(heavy_count * blocks_dev, block_rows, feat_dev)  7.9 us
  transfers between devices with their start and end apart: 2, of which 2 were waited for; matrix products, arithmetic and copies ran while one was open for 7% of the time, Pallas kernels for 0%

commit v1 on v0

v1 whole, which is shorter than its diff:
```python
import functools

import jax
import jax.numpy as jnp
from jax import lax
from jax.experimental import pallas as pl
from jax.experimental.pallas import tpu as pltpu
from jax.sharding import PartitionSpec as P


HEAVY = 3
SMEM = pl.BlockSpec(memory_space=pltpu.SMEM)
VMEM = pl.BlockSpec(memory_space=pltpu.VMEM)


def ring_order(n):
    return list(range(0, n, 2)) + list(range(n - 1, 0, -2))


def ring_place(index, n):
    return jnp.where(index % 2 == 0, index // 2, n - 1 - index // 2)


def wants_kernel(n, blocks_dev, tile_total, cols_ref, want_ref, heavy_ref, mine_ref, seen_ref):
    me = lax.axis_index("rows")

    @pl.loop(0, n)
    def _(o):
        seen_ref[o] = 0

        @pl.loop(0, n)
        def _(p):
            want_ref[o, p] = 0

    @pl.loop(0, tile_total)
    def _(t):
        col = cols_ref[t]
        owner = col // blocks_dev
        seen_ref[owner] = seen_ref[owner] + 1
        want_ref[me, owner] = col % blocks_dev

    def count(o, found):
        return found + ((seen_ref[o] >= 2) & (o != me)).astype(jnp.int32)

    others = lax.fori_loop(0, n, count, 0)
    mine = (others < HEAVY).astype(jnp.int32)
    mine_ref[0] = mine
    for k in range(HEAVY):
        heavy_ref[k] = 0

    def rank(o, found):
        is_heavy = ((seen_ref[o] >= 2) & (o != me)) | ((o == me) & (mine == 1))

        @pl.when(is_heavy)
        def _():
            heavy_ref[jnp.minimum(found, HEAVY - 1)] = o

        return found + is_heavy.astype(jnp.int32)

    lax.fori_loop(0, n, rank, 0)


def find_wants(n, blocks_dev, tile_cols):
    tile_total = tile_cols.shape[0]
    return pl.pallas_call(
        functools.partial(wants_kernel, n, blocks_dev, tile_total),
        out_shape=(
            jax.ShapeDtypeStruct((n, n), jnp.int32),
            jax.ShapeDtypeStruct((HEAVY,), jnp.int32),
            jax.ShapeDtypeStruct((1,), jnp.int32),
        ),
        in_specs=[SMEM],
        out_specs=(SMEM, SMEM, SMEM),
        scratch_shapes=[pltpu.SMEM((n,), jnp.int32)],
        name="wants",
    )(tile_cols)


def order_kernel(
    n, blocks_dev, tile_total, lists, ring, cols_ref, counts_ref, heavy_ref, plan_ref, list_ref, code_ref
):
    me = lax.axis_index("rows")
    here = ring_place(me, n)
    slots = max(n, blocks_dev * (1 if ring else HEAVY))

    @pl.loop(0, lists)
    def _(g):
        plan_ref[g] = 0

    def row_body(j, t0):
        def tile_body(t, carry):
            col = cols_ref[t]
            owner = col // blocks_dev
            local = col % blocks_dev
            heavy_at = jnp.int32(-1)
            for k in range(HEAVY):
                heavy_at = jnp.where(owner == heavy_ref[k], k, heavy_at)
            if ring:
                half = local // n
                there = ring_place(local % n, n)
                hops = jnp.where(half == 0, here - there, there - here)
                hops = jnp.where(hops < 0, hops + n, hops)
                single = (half == 1) & (hops == n - 1) & (heavy_at == HEAVY - 1)
                heavy_list = 2 + 2 * hops + half + single.astype(jnp.int32)
                heavy_slot = jnp.where(single, 0, heavy_at)
            else:
                heavy_list, heavy_slot = 2, heavy_at * blocks_dev + local
            own = owner == me
            which = jnp.where(own, 0, jnp.where(heavy_at < 0, 1, heavy_list))
            slot = jnp.where(own, local, jnp.where(heavy_at < 0, owner, heavy_slot))
            list_ref[t] = which
            plan_ref[which] = plan_ref[which] + 1
            code_ref[t] = (t * blocks_dev + j) * slots + slot
            return carry

        stop = jnp.minimum(t0 + counts_ref[0, j], tile_total)
        lax.fori_loop(t0, stop, tile_body, 0)
        return stop

    lax.fori_loop(0, counts_ref.shape[1], row_body, 0)

    def add_up(g, total):
        count = plan_ref[g]
        plan_ref[g] = total
        return total + count

    lax.fori_loop(0, lists, add_up, 0)

    @pl.loop(0, tile_total)
    def _(t):
        which = list_ref[t]
        at = plan_ref[which]
        plan_ref[which] = at + 1
        plan_ref[lists + at] = code_ref[t]


def order_tiles(n, blocks_dev, lists, ring, tile_cols, row_counts, heavy_ids):
    tile_total = tile_cols.shape[0]
    return pl.pallas_call(
        functools.partial(order_kernel, n, blocks_dev, tile_total, lists, ring),
        out_shape=jax.ShapeDtypeStruct((lists + tile_total,), jnp.int32),
        in_specs=[SMEM] * 3,
        out_specs=SMEM,
        scratch_shapes=[pltpu.SMEM((tile_total,), jnp.int32), pltpu.SMEM((tile_total,), jnp.int32)],
        name="order",
    )(tile_cols, row_counts, heavy_ids)


def pick_kernel(choose, count, *refs):
    index_refs, from_ref, out_ref, sem_ref = refs[:-3], refs[-3], refs[-2], refs[-1]
    copies = [
        pltpu.make_async_copy(from_ref.at[choose(k, *index_refs)], out_ref.at[k], sem_ref.at[k])
        for k in range(count)
    ]
    for copy in copies:
        copy.start()
    for copy in copies:
        copy.wait()


def pick_blocks(choose, count, indices, blocks, to):
    return pl.pallas_call(
        functools.partial(pick_kernel, choose, count),
        out_shape=jax.ShapeDtypeStruct((count, *blocks.shape[1:]), blocks.dtype),
        in_specs=[SMEM] * len(indices) + [VMEM],
        out_specs=pl.BlockSpec(memory_space=to),
        scratch_shapes=[pltpu.SemaphoreType.DMA((count,))],
        compiler_params=pltpu.CompilerParams(vmem_limit_bytes=8 << 20),
        cost_estimate=pl.CostEstimate(
            flops=0, bytes_accessed=8 * count * blocks.shape[1] * blocks.shape[2], transcendentals=0
        ),
        name="pick",
    )(*indices, blocks)


def halves(x):
    high = x.astype(jnp.bfloat16)
    low = (x - high.astype(jnp.float32)).astype(jnp.bfloat16)
    return high, low


def add_kernel(lists, all_lists, slots, first, plan_ref, tiles_ref, *refs):
    panels, out_ref = refs[: len(lists)], refs[-1]
    blocks_dev = out_ref.shape[0]
    if first:
        out_ref[...] = jnp.zeros_like(out_ref)
    for which, panel in zip(lists, panels):
        begin = plan_ref[which - 1] if which else 0

        @pl.loop(begin, plan_ref[which])
        def _(i):
            code = plan_ref[all_lists + i]
            at, slot = code // slots, code % slots
            tile, row = at // blocks_dev, at % blocks_dev
            a_high, a_low = halves(tiles_ref[tile])
            x_high, x_low = halves(jnp.maximum(panel[slot], 0.0))
            left = jnp.concatenate([a_high, a_low, a_high], axis=1)
            right = jnp.concatenate([x_high, x_high, x_low], axis=0)
            out_ref[row] += jnp.dot(left, right, preferred_element_type=jnp.float32)


def add_products(plan, tiles, lists, panels, into, blocks_dev, slots):
    tile_total, block, _ = tiles.shape
    width = panels[0].shape[-1]
    first = into is None
    operands = [plan, tiles, *panels] + ([] if first else [into])
    return pl.pallas_call(
        functools.partial(add_kernel, lists, plan.shape[0] - tile_total, slots, first),
        out_shape=jax.ShapeDtypeStruct((blocks_dev, block, width), jnp.float32),
        in_specs=[SMEM] + [VMEM] * (len(operands) - 1),
        out_specs=VMEM,
        input_output_aliases={} if first else {len(operands) - 1: 0},
        compiler_params=pltpu.CompilerParams(vmem_limit_bytes=24 << 20),
        cost_estimate=pl.CostEstimate(
            flops=20 * len(lists) * block * block * width,
            bytes_accessed=4 * blocks_dev * block * width,
            transcendentals=0,
        ),
        name="add",
    )(*operands)


def per_device(features, norm_gain, row_counts, tile_cols, tile_values):
    node_dev, width = features.shape
    _, block, _ = tile_values.shape
    blocks_dev = node_dev // block
    n = lax.axis_size("rows")
    ring = blocks_dev == 2 * n and n & (n - 1) == 0
    slots = max(n, blocks_dev * (1 if ring else HEAVY))
    blocks = features.reshape(blocks_dev, block, width)
    swap = functools.partial(lax.all_to_all, axis_name="rows", split_axis=0, concat_axis=0, tiled=True)
    tie = lax.optimization_barrier
    if ring:
        lists = 3 + 2 * n
        source, tile_cols = tie((blocks[:n], tile_cols))
        first_part = swap(source)
        want, heavy_ids, mine = find_wants(n, blocks_dev, tile_cols)
        want = lax.psum(want, "rows")

        def second_block(k, want, mine):
            asked = jnp.clip(want[k, lax.axis_index("rows")], 0, blocks_dev - 1)
            return jnp.where(mine[0] == 1, n + k, asked)

        picked = pick_blocks(second_block, n, (want, mine), blocks, pltpu.HBM)
        first_part, picked = tie((first_part, picked))
        second_part = swap(picked)
        order = ring_order(n)
        up = [(order[i], order[(i + 1) % n]) for i in range(n)]
        down = [(b, a) for a, b in up]
        share = functools.partial(pick_blocks, lambda k, ids: ids[k], HEAVY, (heavy_ids,), to=pltpu.VMEM)
        start = share(first_part)
        start, row_counts = tie((start, row_counts))
        plan = order_tiles(n, blocks_dev, lists, True, tile_cols, row_counts, heavy_ids)
        add = functools.partial(add_products, plan, tile_values, blocks_dev=blocks_dev, slots=slots)
        ahead = lax.ppermute(start, "rows", up)
        total = add((0, 2), (blocks, start), None)
        second_part, total = tie((second_part, total))
        mine_back = share(second_part)
        back = mine_back
        ready = [(1, second_part), (3, back), (4, ahead)]
        for hop in range(1, n - 1):
            back = lax.ppermute(back, "rows", down)
            ahead = lax.ppermute(ahead, "rows", up)
            total = add(tuple(g for g, _ in ready), tuple(p for _, p in ready), total)
            ahead, total = tie((ahead, total))
            ready = [(3 + 2 * hop, back), (4 + 2 * hop, ahead)]
        third = HEAVY - 1
        back = lax.ppermute(back[third:], "rows", down)
        straight = lax.ppermute(mine_back[:third], "rows", up)
        total = add(tuple(g for g, _ in ready), tuple(p for _, p in ready), total)
        straight, total = tie((straight, total))
        total = add((2 * n + 1, 2 * n + 2), (straight, back), total)
    else:
        want, heavy_ids, mine = find_wants(n, blocks_dev, tile_cols)
        me = lax.axis_index("rows")
        asked = swap(want[me].reshape(n, 1))[:, 0]
        plan = order_tiles(n, blocks_dev, 3, False, tile_cols, row_counts, heavy_ids)
        piece = node_dev // n
        light = swap(blocks[asked])
        scattered = swap(features.reshape(n, piece, width))[heavy_ids]
        heavy = lax.all_gather(scattered, "rows", axis=1, tiled=True).reshape(HEAVY * blocks_dev, block, width)
        total = add_products(plan, tile_values, (0, 1, 2), (blocks, light, heavy), None, blocks_dev, slots)
    aggregate = total.reshape(node_dev, width)
    square_sum = jnp.sum(lax.all_gather(jnp.sum(aggregate * aggregate, axis=1), "feat"), axis=0)
    mean_square = square_sum / (width * lax.axis_size("feat"))
    return aggregate * norm_gain[None, :] * lax.rsqrt(mean_square + 1e-05)[:, None]


def solution(mesh):
    placed = (P("rows", "feat"), P("feat"), P("rows", None), P("rows"), P("rows", None, None))
    return jax.shard_map(per_device, mesh=mesh, in_specs=placed, out_specs=P("rows", "feat"), check_vma=False)
```

time: 342 us -> 146 us (0.43)
  waiting for transfers between devices: 194 us -> 28.7 us
  Pallas kernels: 0 us -> 35.9 us
  local copies, waits for them, and re-layouts: 50.5 us -> 15.6 us
  starting transfers between devices: 3.56 us -> 34.8 us
  matrix products: 26.6 us -> 0 us
  other arithmetic: 23.2 us -> 2.04 us
  between operations: 15.5 us -> 0.23 us
    psum x1 -> x0, waiting for transfers between devices: 158 us -> none  [broadcast(): return lax.psum(block, axis)]
    pallas_call x0 -> x14, Pallas kernels: none -> 35.9 us  [the longest x9 22.5 us: add_products(): pl.pallas_call(functools.partial(add_kernel, lists, plan.shape[0] - tile_...]
    all_to_all x1 -> x2, waiting for transfers between devices: 35.4 us -> 6.15 us  [the longest x1 6.15 us: per_device(): second_part = swap(picked)]
    dot_general x4 -> x0, matrix products: 26.6 us -> none  [the longest x1 15.2 us: per_device(): jnp.einsum('tij,tjf->tif', tile_values[ranking], picked, precision=lax.Pr...]
    gather x7 -> x0, local copies, waits for them, and re-layouts: 25.3 us -> none  [the longest x1 11.7 us: per_device(): picked = near_panel[near_slot]]
    ppermute x0 -> x15, starting transfers between devices: none -> 23.9 us  [the longest x6 13.2 us: per_device(): ahead = lax.ppermute(ahead, 'rows', up)]
    ppermute x0 -> x15, waiting for transfers between devices: none -> 22.5 us  [the longest x6 13.7 us: per_device(): ahead = lax.ppermute(ahead, 'rows', up)]
    psum x1, blocking collectives: 6.35 us -> 22.8 us  [per_device(): want = lax.psum(want, 'rows')]
  transfers between devices with their start and end apart: 2 -> 17, of which waited for: 2 -> 11; matrix products, arithmetic and copies ran while one was open for 7% -> 0% of each run, Pallas kernels for 0% -> 24%
where the time goes in v1:
time: 146 us; the launch traced here: 145 us
  Pallas kernels  35.9 us (25%)
  starting transfers between devices  34.8 us (24%)
  waiting for transfers between devices  28.7 us (20%)
  blocking collectives  28 us (19%)
  local copies, waits for them, and re-layouts  15.6 us (11%)
  other arithmetic  2.04 us (1%)
    psum x1, blocking collectives, per_device(): want = lax.psum(want, 'rows')  22.8 us
    pallas_call x9, Pallas kernels, add_products(): pl.pallas_call(functools.partial(add_kernel, lists, plan.shape[0] - tile_...  22.5 us
    ppermute x6, waiting for transfers between devices, per_device(): ahead = lax.ppermute(ahead, 'rows', up)  13.7 us
    ppermute x6, starting transfers between devices, per_device(): ahead = lax.ppermute(ahead, 'rows', up)  13.2 us
    unnamed x26, local copies, waits for them, and re-layouts  13.1 us
    ppermute x6, waiting for transfers between devices, per_device(): back = lax.ppermute(back, 'rows', down)  7.99 us
    all_to_all x1, starting transfers between devices, per_device(): first_part = swap(source)  7.28 us
    all_to_all x1, waiting for transfers between devices, per_device(): second_part = swap(picked)  6.15 us
  transfers between devices with their start and end apart: 17, of which 11 were waited for; matrix products, arithmetic and copies ran while one was open for 0% of the time, Pallas kernels for 24%

profile of v1, /device:TPU:0, one launch (start us, length us, event | category | flops | bytes accessed | tf_op | source)
XLA Modules:
  0.0 145.3 jit_solution(18396488799528587153)
XLA Ops:
  2.4 7.3 %all-to-all-start = ((f32[8,128,256]{2,1,0:T(8,128)}), f32[8,128,256]{2,1,0:T(8,128)S(1)}, u32[]{:S(2)}, u32[]{:S(2)}) async-start(f32[8,128,256]{2,1,0:T(8,128)} %bitcast.9), calls=%async_computation | async-start | bytes 2097152 | tf_op jit(solution)/shard_map/all_to_all | solution.py:236
  9.7 3.2 %wants.1 = (s32[8,8]{1,0:T(8,128)}, s32[3]{0:T(128)}, s32[1]{0:T(128)}) custom-call(s32[86]{0:T(128)} %cols_ref.1), custom_call_target="tpu_custom_call" | custom-call | tf_op jit(solution)/shard_map/wants/pallas_call | solution.py:65
  12.9 22.8 %psum.7.refs_0_ = s32[8,8]{1,0:T(8,128)S(1)} all-reduce(s32[8,8]{1,0:T(8,128)} %get-tuple-element.33), channel_id=1, replica_groups=mesh['rows'=8,'feat'=4] {'rows'}, use_global_device_ids=true, to_apply=%region_0.0 | all-reduce | flops 64 | bytes 512 | tf_op jit(solution)/shard_map/psum | solution.py:238
  35.7 2.7 %pick.3 = f32[8,128,256]{2,1,0:T(8,128)S(1)} custom-call(s32[8,8]{1,0:T(8,128)S(1)} %psum.7.refs_0_, s32[1]{0:T(128)} %get-tuple-element.34.refs_1_, f32[16,128,256]{2,1,0:T(8,128)S(1)} %bitcast.7), custom_call_target="tpu_custom_call" | custom-call | bytes 2097152 | tf_op jit(solution)/shard_map/pick/pallas_call | solution.py:162
  40.3 3.6 %all-to-all-start.1 = ((f32[8,128,256]{2,1,0:T(8,128)}), f32[8,128,256]{2,1,0:T(8,128)S(1)}, u32[]{:S(2)}, u32[]{:S(2)}) async-start(f32[8,128,256]{2,1,0:T(8,128)} %copy-done.7), calls=%async_computation.1 | async-start | bytes 2097152 | tf_op jit(solution)/shard_map/all_to_all | solution.py:246
  48.3 5.4 %order.1.plan_ref = s32[105]{0:T(128)} custom-call(s32[86]{0:T(128)} %cols_ref.1, s32[1,16]{1,0:T(1,128)} %counts_ref, s32[3]{0:T(128)} %get-tuple-element.31.refs_0_.heavy_ref), custom_call_target="tpu_custom_call" | custom-call | tf_op jit(solution)/shard_map/order/pallas_call | solution.py:139
  53.8 2.6 %copy-done = f32[86,128,128]{2,1,0:T(8,128)S(1)} copy-done((f32[86,128,128]{2,1,0:T(8,128)S(1)}, f32[86,128,128]{2,1,0:T(8,128)}, u32[]{:S(2)}) %copy-start) | copy-done | bytes 5636120
  58.5 5.2 %add.25.refs_3_ = f32[16,128,256]{2,1,0:T(8,128)S(1)} custom-call(s32[105]{0:T(128)S(1)} %copy-done.8, f32[86,128,128]{2,1,0:T(8,128)S(1)} %copy-done, f32[16,128,256]{2,1,0:T(8,128)S(1)} %bitcast.8, f32[3,128,256]{2,1,0:T(8,128)S(1)} %pick.4.refs_1_), custom_call_target="tpu_custom_call" | custom-call | flops 167772160 | bytes 2097152 | tf_op jit(solution)/shard_map/add/pallas_call | solution.py:207
  63.7 6.1 %all-to-all-done.1.refs_1_.refs_0_ = f32[8,128,256]{2,1,0:T(8,128)S(1)} async-done(((f32[8,128,256]{2,1,0:T(8,128)}), f32[8,128,256]{2,1,0:T(8,128)S(1)}, u32[]{:S(2)}, u32[]{:S(2)}) %all-to-all-start.1) | async-done | bytes 1048608 | tf_op jit(solution)/shard_map/all_to_all | solution.py:246
  73.4 3.6 %collective-permute-start.8 = (f32[3,128,256]{2,1,0:T(8,128)}, f32[3,128,256]{2,1,0:T(8,128)S(1)}, u32[]{:S(2)}, u32[]{:S(2)}) collective-permute-start(f32[3,128,256]{2,1,0:T(8,128)} %collective-permute-done.7.refs_2_), channel_id=1, source_target_pairs={{0,8},{8,16},{16,24},{24,28},{28,20},{20,12},{12,4},{4,0},{1,9},{9... | collective-permute-start | bytes 1179656 | tf_op jit(solution)/shard_map/ppermute | solution.py:263
  77.1 3.9 %collective-permute-done.1.refs_0_ = f32[3,128,256]{2,1,0:T(8,128)S(1)} collective-permute-done((f32[3,128,256]{2,1,0:T(8,128)S(1)}, f32[3,128,256]{2,1,0:T(8,128)S(1)}, u32[]{:S(2)}, u32[]{:S(2)}) %collective-permute-start.1) | collective-permute-done | bytes 393248 | tf_op jit(solution)/shard_map/ppermute | solution.py:262
  82.7 2.6 %copy-done.1 = f32[86,128,128]{2,1,0:T(8,128)S(1)} copy-done((f32[86,128,128]{2,1,0:T(8,128)S(1)}, f32[86,128,128]{2,1,0:T(8,128)}, u32[]{:S(2)}) %copy-start.1) | copy-done | bytes 5636120
  85.3 3.0 %add.26.refs_2_ = f32[16,128,256]{2,1,0:T(8,128)S(1)} custom-call(s32[105]{0:T(128)S(1)} %copy-done.9, f32[86,128,128]{2,1,0:T(8,128)S(1)} %copy-done.1, f32[8,128,256]{2,1,0:T(8,128)S(1)} %all-to-all-done.1.refs_1_.refs_0_, f32[3,128,256]{2,1,0:T(8,128)S(1)} %pick.5.refs_1_, ...), custom_call_target="tpu_custom_call", output_to_operand_aliasing={{}: (5, {})} | custom-call | flops 251658240 | bytes 2097152 | tf_op jit(solution)/shard_map/add/pallas_call | solution.py:207
  91.7 2.6 %copy-done.2 = f32[86,128,128]{2,1,0:T(8,128)S(1)} copy-done((f32[86,128,128]{2,1,0:T(8,128)S(1)}, f32[86,128,128]{2,1,0:T(8,128)}, u32[]{:S(2)}) %copy-start.2) | copy-done | bytes 5636120
  94.3 2.5 %add.27.refs_2_ = f32[16,128,256]{2,1,0:T(8,128)S(1)} custom-call(s32[105]{0:T(128)S(1)} %copy-done.9, f32[86,128,128]{2,1,0:T(8,128)S(1)} %copy-done.2, f32[3,128,256]{2,1,0:T(8,128)S(1)} %collective-permute-done.1.refs_0_, f32[3,128,256]{2,1,0:T(8,128)S(1)} %collective-permute-done.8.refs_1_, ...), custom_call_target="tpu_custom_call", output_to_operand_aliasing={{}: (4, {})} | custom-call | flops 167772160 | bytes 2097152 | tf_op jit(solution)/shard_map/add/pallas_call | solution.py:207
  99.7 2.7 %add.28.refs_2_ = f32[16,128,256]{2,1,0:T(8,128)S(1)} custom-call(s32[105]{0:T(128)S(1)} %copy-done.9, f32[86,128,128]{2,1,0:T(8,128)S(1)} %copy-done.2, f32[3,128,256]{2,1,0:T(8,128)S(1)} %collective-permute-done.2.refs_0_, f32[3,128,256]{2,1,0:T(8,128)S(1)} %collective-permute-done.9.refs_1_, ...), custom_call_target="tpu_custom_call", output_to_operand_aliasing={{}: (4, {})} | custom-call | flops 167772160 | bytes 2097152 | tf_op jit(solution)/shard_map/add/pallas_call | solution.py:207
  102.4 3.1 %collective-permute-done.10.refs_1_ = f32[3,128,256]{2,1,0:T(8,128)S(1)} collective-permute-done((f32[3,128,256]{2,1,0:T(8,128)S(1)}, f32[3,128,256]{2,1,0:T(8,128)S(1)}, u32[]{:S(2)}, u32[]{:S(2)}) %collective-permute-start.10) | collective-permute-done | bytes 393248 | tf_op jit(solution)/shard_map/ppermute | solution.py:263
  105.6 2.5 %collective-permute-start.11 = (f32[3,128,256]{2,1,0:T(8,128)S(1)}, f32[3,128,256]{2,1,0:T(8,128)S(1)}, u32[]{:S(2)}, u32[]{:S(2)}) collective-permute-start(f32[3,128,256]{2,1,0:T(8,128)S(1)} %collective-permute-done.10.refs_1_), channel_id=1, source_target_pairs={{0,8},{8,16},{16,24},{24,28},{28,20},{20,12},{12,4},{4,0},{1,9},{9... | collective-permute-start | bytes 1179656 | tf_op jit(solution)/shard_map/ppermute | solution.py:263
  110.9 3.9 %collective-permute-done.11.refs_1_ = f32[3,128,256]{2,1,0:T(8,128)S(1)} collective-permute-done((f32[3,128,256]{2,1,0:T(8,128)S(1)}, f32[3,128,256]{2,1,0:T(8,128)S(1)}, u32[]{:S(2)}, u32[]{:S(2)}) %collective-permute-start.11) | collective-permute-done | bytes 393248 | tf_op jit(solution)/shard_map/ppermute | solution.py:263
  120.3 4.1 %collective-permute-done.12.refs_1_ = f32[3,128,256]{2,1,0:T(8,128)S(1)} collective-permute-done((f32[3,128,256]{2,1,0:T(8,128)S(1)}, f32[3,128,256]{2,1,0:T(8,128)S(1)}, u32[]{:S(2)}, u32[]{:S(2)}) %collective-permute-start.12) | collective-permute-done | bytes 393248 | tf_op jit(solution)/shard_map/ppermute | solution.py:263
  124.4 2.6 %collective-permute-start.13 = (f32[3,128,256]{2,1,0:T(8,128)S(1)}, f32[3,128,256]{2,1,0:T(8,128)S(1)}, u32[]{:S(2)}, u32[]{:S(2)}) collective-permute-start(f32[3,128,256]{2,1,0:T(8,128)S(1)} %collective-permute-done.12.refs_1_), channel_id=1, source_target_pairs={{0,8},{8,16},{16,24},{24,28},{28,20},{20,12},{12,4},{4,0},{1,9},{9... | collective-permute-start | bytes 1179656 | tf_op jit(solution)/shard_map/ppermute | solution.py:263
  127.0 2.5 %collective-permute-start = (f32[2,128,256]{2,1,0:T(8,128)S(1)}, f32[2,128,256]{2,1,0:T(8,128)S(1)}, u32[]{:S(2)}, u32[]{:S(2)}) collective-permute-start(f32[2,128,256]{2,1,0:T(8,128)S(1)} %slice.16), channel_id=1, source_target_pairs={{0,8},{8,16},{16,24},{24,28},{28,20},{20,12},{12,4},{4,0},{1,9},{9... | collective-permute-start | bytes 786440 | tf_op jit(solution)/shard_map/ppermute | solution.py:269
  131.3 2.5 %collective-permute-done.13.refs_1_ = f32[3,128,256]{2,1,0:T(8,128)S(1)} collective-permute-done((f32[3,128,256]{2,1,0:T(8,128)S(1)}, f32[3,128,256]{2,1,0:T(8,128)S(1)}, u32[]{:S(2)}, u32[]{:S(2)}) %collective-permute-start.13) | collective-permute-done | bytes 393248 | tf_op jit(solution)/shard_map/ppermute | solution.py:263
  138.4 5.2 %all-gather = f32[4,1,2048]{2,1,0:T(1,128)S(1)} all-gather(f32[1,1,2048]{2,1,0:T(1,128)S(1)} %bitcast.10), channel_id=1, replica_groups=mesh['rows'=8,'feat'=4] {'feat'}, dimensions={0}, use_global_device_ids=true | all-gather | bytes 40960 | tf_op jit(solution)/shard_map/all_gather | solution.py:284
  (59 shorter events, 38.8 us)
Async XLA Ops:
  0.0 35.7 %copy-start.3 = (f32[2048,256]{1,0:T(8,128)S(1)}, f32[2048,256]{1,0:T(8,128)}, u32[]{:S(2)}) copy-start(f32[2048,256]{1,0:T(8,128)} %param.5) | copy-start | bytes 6291460
  2.4 36.9 %all-to-all-start = ((f32[8,128,256]{2,1,0:T(8,128)}), f32[8,128,256]{2,1,0:T(8,128)S(1)}, u32[]{:S(2)}, u32[]{:S(2)}) async-start(f32[8,128,256]{2,1,0:T(8,128)} %bitcast.9), calls=%async_computation | async-start | bytes 2097152 | tf_op jit(solution)/shard_map/all_to_all | solution.py:236
  35.7 8.3 %copy-start.10 = (s32[3]{0:T(128)S(1)}, s32[3]{0:T(128)}, u32[]{:S(2)}) copy-start(s32[3]{0:T(128)} %get-tuple-element.31.refs_0_.heavy_ref) | copy-start | bytes 40
  40.3 29.5 %all-to-all-start.1 = ((f32[8,128,256]{2,1,0:T(8,128)}), f32[8,128,256]{2,1,0:T(8,128)S(1)}, u32[]{:S(2)}, u32[]{:S(2)}) async-start(f32[8,128,256]{2,1,0:T(8,128)} %copy-done.7), calls=%async_computation.1 | async-start | bytes 2097152 | tf_op jit(solution)/shard_map/all_to_all | solution.py:246
  46.3 27.2 %collective-permute-start.7 = (f32[3,128,256]{2,1,0:T(8,128)S(1)}, f32[3,128,256]{2,1,0:T(8,128)}, u32[]{:S(2)}, u32[]{:S(2)}) collective-permute-start(f32[3,128,256]{2,1,0:T(8,128)S(1)} %pick.4.refs_1_), channel_id=1, source_target_pairs={{0,8},{8,16},{16,24},{24,28},{28,20},{20,12},{12,4},{4,0},{1,9},{9... | collective-permute-start | bytes 1179656 | tf_op jit(solution)/shard_map/ppermute | solution.py:255
  53.7 2.6 %copy-start = (f32[86,128,128]{2,1,0:T(8,128)S(1)}, f32[86,128,128]{2,1,0:T(8,128)}, u32[]{:S(2)}) copy-start(f32[86,128,128]{2,1,0:T(8,128)} %tiles_ref.17) | copy-start | bytes 16908292
  58.5 11.4 %copy-start.11 = (s32[3]{0:T(128)S(1)}, s32[3]{0:T(128)}, u32[]{:S(2)}) copy-start(s32[3]{0:T(128)} %get-tuple-element.31.refs_0_.heavy_ref) | copy-start | bytes 40
  58.5 24.2 %copy-start.9 = (s32[105]{0:T(128)S(1)}, s32[105]{0:T(128)}, u32[]{:S(2)}) copy-start(s32[105]{0:T(128)} %order.1.plan_ref) | copy-start | bytes 1264
  71.0 10.0 %collective-permute-start.1 = (f32[3,128,256]{2,1,0:T(8,128)S(1)}, f32[3,128,256]{2,1,0:T(8,128)S(1)}, u32[]{:S(2)}, u32[]{:S(2)}) collective-permute-start(f32[3,128,256]{2,1,0:T(8,128)S(1)} %pick.5.refs_1_), channel_id=1, source_target_pairs={{8,0},{16,8},{24,16},{28,24},{20,28},{12,20},{4,12},{0,4},{9,1},{1... | collective-permute-start | bytes 1179656 | tf_op jit(solution)/shard_map/ppermute | solution.py:262
  73.4 14.9 %collective-permute-start.8 = (f32[3,128,256]{2,1,0:T(8,128)}, f32[3,128,256]{2,1,0:T(8,128)S(1)}, u32[]{:S(2)}, u32[]{:S(2)}) collective-permute-start(f32[3,128,256]{2,1,0:T(8,128)} %collective-permute-done.7.refs_2_), channel_id=1, source_target_pairs={{0,8},{8,16},{16,24},{24,28},{28,20},{20,12},{12,4},{4,0},{1,9},{9... | collective-permute-start | bytes 1179656 | tf_op jit(solution)/shard_map/ppermute | solution.py:263
  81.0 9.1 %collective-permute-start.2 = (f32[3,128,256]{2,1,0:T(8,128)S(1)}, f32[3,128,256]{2,1,0:T(8,128)S(1)}, u32[]{:S(2)}, u32[]{:S(2)}) collective-permute-start(f32[3,128,256]{2,1,0:T(8,128)S(1)} %collective-permute-done.1.refs_0_), channel_id=1, source_target_pairs={{8,0},{16,8},{24,16},{28,24},{20,28},{12,20},{4,12},{0,4},{9,1},{1... | collective-permute-start | bytes 1179656 | tf_op jit(solution)/shard_map/ppermute | solution.py:262
  82.7 2.6 %copy-start.1 = (f32[86,128,128]{2,1,0:T(8,128)S(1)}, f32[86,128,128]{2,1,0:T(8,128)}, u32[]{:S(2)}) copy-start(f32[86,128,128]{2,1,0:T(8,128)} %tiles_ref.17) | copy-start | bytes 16908292
  88.3 8.5 %collective-permute-start.9 = (f32[3,128,256]{2,1,0:T(8,128)S(1)}, f32[3,128,256]{2,1,0:T(8,128)S(1)}, u32[]{:S(2)}, u32[]{:S(2)}) collective-permute-start(f32[3,128,256]{2,1,0:T(8,128)S(1)} %collective-permute-done.8.refs_1_), channel_id=1, source_target_pairs={{0,8},{8,16},{16,24},{24,28},{28,20},{20,12},{12,4},{4,0},{1,9},{9... | collective-permute-start | bytes 1179656 | tf_op jit(solution)/shard_map/ppermute | solution.py:263
  90.1 9.6 %collective-permute-start.3 = (f32[3,128,256]{2,1,0:T(8,128)S(1)}, f32[3,128,256]{2,1,0:T(8,128)S(1)}, u32[]{:S(2)}, u32[]{:S(2)}) collective-permute-start(f32[3,128,256]{2,1,0:T(8,128)S(1)} %collective-permute-done.2.refs_0_), channel_id=1, source_target_pairs={{8,0},{16,8},{24,16},{28,24},{20,28},{12,20},{4,12},{0,4},{9,1},{1... | collective-permute-start | bytes 1179656 | tf_op jit(solution)/shard_map/ppermute | solution.py:262
  96.8 8.7 %collective-permute-start.10 = (f32[3,128,256]{2,1,0:T(8,128)S(1)}, f32[3,128,256]{2,1,0:T(8,128)S(1)}, u32[]{:S(2)}, u32[]{:S(2)}) collective-permute-start(f32[3,128,256]{2,1,0:T(8,128)S(1)} %collective-permute-done.9.refs_1_), channel_id=1, source_target_pairs={{0,8},{8,16},{16,24},{24,28},{28,20},{20,12},{12,4},{4,0},{1,9},{9... | collective-permute-start | bytes 1179656 | tf_op jit(solution)/shard_map/ppermute | solution.py:263
  99.7 9.1 %collective-permute-start.4 = (f32[3,128,256]{2,1,0:T(8,128)S(1)}, f32[3,128,256]{2,1,0:T(8,128)S(1)}, u32[]{:S(2)}, u32[]{:S(2)}) collective-permute-start(f32[3,128,256]{2,1,0:T(8,128)S(1)} %collective-permute-done.3.refs_0_), channel_id=1, source_target_pairs={{8,0},{16,8},{24,16},{28,24},{20,28},{12,20},{4,12},{0,4},{9,1},{1... | collective-permute-start | bytes 1179656 | tf_op jit(solution)/shard_map/ppermute | solution.py:262
  105.6 9.3 %collective-permute-start.11 = (f32[3,128,256]{2,1,0:T(8,128)S(1)}, f32[3,128,256]{2,1,0:T(8,128)S(1)}, u32[]{:S(2)}, u32[]{:S(2)}) collective-permute-start(f32[3,128,256]{2,1,0:T(8,128)S(1)} %collective-permute-done.10.refs_1_), channel_id=1, source_target_pairs={{0,8},{8,16},{16,24},{24,28},{28,20},{20,12},{12,4},{4,0},{1,9},{9... | collective-permute-start | bytes 1179656 | tf_op jit(solution)/shard_map/ppermute | solution.py:263
  108.8 9.2 %collective-permute-start.5 = (f32[3,128,256]{2,1,0:T(8,128)S(1)}, f32[3,128,256]{2,1,0:T(8,128)S(1)}, u32[]{:S(2)}, u32[]{:S(2)}) collective-permute-start(f32[3,128,256]{2,1,0:T(8,128)S(1)} %collective-permute-done.4.refs_0_), channel_id=1, source_target_pairs={{8,0},{16,8},{24,16},{28,24},{20,28},{12,20},{4,12},{0,4},{9,1},{1... | collective-permute-start | bytes 1179656 | tf_op jit(solution)/shard_map/ppermute | solution.py:262
  114.8 9.5 %collective-permute-start.12 = (f32[3,128,256]{2,1,0:T(8,128)S(1)}, f32[3,128,256]{2,1,0:T(8,128)S(1)}, u32[]{:S(2)}, u32[]{:S(2)}) collective-permute-start(f32[3,128,256]{2,1,0:T(8,128)S(1)} %collective-permute-done.11.refs_1_), channel_id=1, source_target_pairs={{0,8},{8,16},{16,24},{24,28},{28,20},{20,12},{12,4},{4,0},{1,9},{9... | collective-permute-start | bytes 1179656 | tf_op jit(solution)/shard_map/ppermute | solution.py:263
  118.1 11.4 %collective-permute-start.6 = (f32[3,128,256]{2,1,0:T(8,128)S(1)}, f32[3,128,256]{2,1,0:T(8,128)S(1)}, u32[]{:S(2)}, u32[]{:S(2)}) collective-permute-start(f32[3,128,256]{2,1,0:T(8,128)S(1)} %collective-permute-done.5.refs_0_), channel_id=1, source_target_pairs={{8,0},{16,8},{24,16},{28,24},{20,28},{12,20},{4,12},{0,4},{9,1},{1... | collective-permute-start | bytes 1179656 | tf_op jit(solution)/shard_map/ppermute | solution.py:262
  124.4 9.5 %collective-permute-start.13 = (f32[3,128,256]{2,1,0:T(8,128)S(1)}, f32[3,128,256]{2,1,0:T(8,128)S(1)}, u32[]{:S(2)}, u32[]{:S(2)}) collective-permute-start(f32[3,128,256]{2,1,0:T(8,128)S(1)} %collective-permute-done.12.refs_1_), channel_id=1, source_target_pairs={{0,8},{8,16},{16,24},{24,28},{28,20},{20,12},{12,4},{4,0},{1,9},{9... | collective-permute-start | bytes 1179656 | tf_op jit(solution)/shard_map/ppermute | solution.py:263
  127.0 9.7 %collective-permute-start = (f32[2,128,256]{2,1,0:T(8,128)S(1)}, f32[2,128,256]{2,1,0:T(8,128)S(1)}, u32[]{:S(2)}, u32[]{:S(2)}) collective-permute-start(f32[2,128,256]{2,1,0:T(8,128)S(1)} %slice.16), channel_id=1, source_target_pairs={{0,8},{8,16},{16,24},{24,28},{28,20},{20,12},{12,4},{4,0},{1,9},{9... | collective-permute-start | bytes 786440 | tf_op jit(solution)/shard_map/ppermute | solution.py:269
  129.5 7.1 %collective-permute-start.14 = (f32[1,128,256]{2,1,0:T(8,128)S(1)}, f32[1,128,256]{2,1,0:T(8,128)S(1)}, u32[]{:S(2)}, u32[]{:S(2)}) collective-permute-start(f32[1,128,256]{2,1,0:T(8,128)S(1)} %slice.17), channel_id=1, source_target_pairs={{8,0},{16,8},{24,16},{28,24},{20,28},{12,20},{4,12},{0,4},{9,1},{1... | collective-permute-start | bytes 393224 | tf_op jit(solution)/shard_map/ppermute | solution.py:268
  138.0 5.6 %copy-start.12 = (f32[256]{0:T(256)S(1)}, f32[256]{0:T(256)}, u32[]{:S(2)}) copy-start(f32[256]{0:T(256)} %param.6) | copy-start | bytes 3076
  (6 other events, 8.0 us)

commit v2 on v1

--- a/solution.py
+++ b/solution.py
@@ -10,6 +10,7 @@
 
 HEAVY = 3
 SMEM = pl.BlockSpec(memory_space=pltpu.SMEM)
+HBM = pl.BlockSpec(memory_space=pltpu.HBM)
 VMEM = pl.BlockSpec(memory_space=pltpu.VMEM)
 
 
@@ -21,23 +22,23 @@
     return jnp.where(index % 2 == 0, index // 2, n - 1 - index // 2)
 
 
-def wants_kernel(n, blocks_dev, tile_total, cols_ref, want_ref, heavy_ref, mine_ref, seen_ref):
+def find_heavy(n, blocks_dev, tile_total, cols_ref, heavy_ref, mine_ref, seen_ref, last_ref):
     me = lax.axis_index("rows")
 
     @pl.loop(0, n)
     def _(o):
         seen_ref[o] = 0
-
-        @pl.loop(0, n)
-        def _(p):
-            want_ref[o, p] = 0
+        last_ref[o] = 0
 
     @pl.loop(0, tile_total)
     def _(t):
         col = cols_ref[t]
         owner = col // blocks_dev
         seen_ref[owner] = seen_ref[owner] + 1
-        want_ref[me, owner] = col % blocks_dev
+        last_ref[owner] = col % blocks_dev
+
+    for k in range(HEAVY):
+        heavy_ref[k] = 0
 
     def count(o, found):
         return found + ((seen_ref[o] >= 2) & (o != me)).astype(jnp.int32)
@@ -45,8 +46,6 @@
     others = lax.fori_loop(0, n, count, 0)
     mine = (others < HEAVY).astype(jnp.int32)
     mine_ref[0] = mine
-    for k in range(HEAVY):
-        heavy_ref[k] = 0
 
     def rank(o, found):
         is_heavy = ((seen_ref[o] >= 2) & (o != me)) | ((o == me) & (mine == 1))
@@ -60,20 +59,68 @@
     lax.fori_loop(0, n, rank, 0)
 
 
+def wants_kernel(n, blocks_dev, tile_total, cols_ref, heavy_ref, mine_ref, want_ref, seen_ref):
+    find_heavy(n, blocks_dev, tile_total, cols_ref, heavy_ref, mine_ref, seen_ref, want_ref)
+
+
 def find_wants(n, blocks_dev, tile_cols):
     tile_total = tile_cols.shape[0]
+    ints = lambda count: jax.ShapeDtypeStruct((count,), jnp.int32)
     return pl.pallas_call(
         functools.partial(wants_kernel, n, blocks_dev, tile_total),
-        out_shape=(
-            jax.ShapeDtypeStruct((n, n), jnp.int32),
-            jax.ShapeDtypeStruct((HEAVY,), jnp.int32),
-            jax.ShapeDtypeStruct((1,), jnp.int32),
-        ),
+        out_shape=(ints(HEAVY), ints(1), ints(n)),
         in_specs=[SMEM],
-        out_specs=(SMEM, SMEM, SMEM),
+        out_specs=(SMEM,) * 3,
         scratch_shapes=[pltpu.SMEM((n,), jnp.int32)],
         name="wants",
     )(tile_cols)
+
+
+def head_kernel(
+    n, blocks_dev, tile_total, cols_ref, from_ref,
+    heavy_ref, mine_ref, want_ref, half_ref,
+    seen_ref, last_ref, buf_ref, in_sem, out_sem,
+):
+    ins = [pltpu.make_async_copy(from_ref.at[k], buf_ref.at[k], in_sem.at[k]) for k in range(n)]
+    outs = [pltpu.make_async_copy(buf_ref.at[k], half_ref.at[k], out_sem.at[k]) for k in range(n)]
+    for copy in ins:
+        copy.start()
+    me = lax.axis_index("rows")
+    for o in range(n):
+        for p in range(n):
+            want_ref[o, p] = 0
+    for copy, onward in zip(ins, outs):
+        copy.wait()
+        onward.start()
+    find_heavy(n, blocks_dev, tile_total, cols_ref, heavy_ref, mine_ref, seen_ref, last_ref)
+    for p in range(n):
+        want_ref[me, p] = last_ref[p]
+    for copy in outs:
+        copy.wait()
+
+
+def start_up(n, blocks_dev, tile_cols, blocks):
+    tile_total = tile_cols.shape[0]
+    shape = (n, *blocks.shape[1:])
+    return pl.pallas_call(
+        functools.partial(head_kernel, n, blocks_dev, tile_total),
+        out_shape=(
+            jax.ShapeDtypeStruct((HEAVY,), jnp.int32),
+            jax.ShapeDtypeStruct((1,), jnp.int32),
+            jax.ShapeDtypeStruct((n, n), jnp.int32),
+            pltpu.HBM(shape, jnp.float32),
+        ),
+        in_specs=[SMEM, HBM],
+        out_specs=(SMEM, SMEM, SMEM, HBM),
+        scratch_shapes=[
+            pltpu.SMEM((n,), jnp.int32),
+            pltpu.SMEM((n,), jnp.int32),
+            pltpu.VMEM(shape, jnp.float32),
+            pltpu.SemaphoreType.DMA((n,)),
+            pltpu.SemaphoreType.DMA((n,)),
+        ],
+        name="head",
+    )(tile_cols, blocks)
 
 
 def order_kernel(
@@ -100,9 +147,7 @@
                 there = ring_place(local % n, n)
                 hops = jnp.where(half == 0, here - there, there - here)
                 hops = jnp.where(hops < 0, hops + n, hops)
-                single = (half == 1) & (hops == n - 1) & (heavy_at == HEAVY - 1)
-                heavy_list = 2 + 2 * hops + half + single.astype(jnp.int32)
-                heavy_slot = jnp.where(single, 0, heavy_at)
+                heavy_list, heavy_slot = 2 + 2 * hops + half, heavy_at
             else:
                 heavy_list, heavy_slot = 2, heavy_at * blocks_dev + local
             own = owner == me
@@ -158,11 +203,11 @@
         copy.wait()
 
 
-def pick_blocks(choose, count, indices, blocks, to):
+def pick_blocks(choose, count, indices, blocks, at, to):
     return pl.pallas_call(
         functools.partial(pick_kernel, choose, count),
-        out_shape=jax.ShapeDtypeStruct((count, *blocks.shape[1:]), blocks.dtype),
-        in_specs=[SMEM] * len(indices) + [VMEM],
+        out_shape=to((count, *blocks.shape[1:]), blocks.dtype),
+        in_specs=[SMEM] * len(indices) + [pl.BlockSpec(memory_space=at)],
         out_specs=pl.BlockSpec(memory_space=to),
         scratch_shapes=[pltpu.SemaphoreType.DMA((count,))],
         compiler_params=pltpu.CompilerParams(vmem_limit_bytes=8 << 20),
@@ -180,10 +225,17 @@
 
 
 def add_kernel(lists, all_lists, slots, first, plan_ref, tiles_ref, *refs):
-    panels, out_ref = refs[: len(lists)], refs[-1]
+    panels = refs[: len(lists)]
+    if first:
+        out_ref, kept_ref, sem_ref = refs[len(lists):]
+        bring = pltpu.make_async_copy(tiles_ref, kept_ref, sem_ref)
+        bring.start()
+        out_ref[...] = jnp.zeros_like(out_ref)
+        bring.wait()
+        tiles_ref = kept_ref
+    else:
+        out_ref = refs[-1]
     blocks_dev = out_ref.shape[0]
-    if first:
-        out_ref[...] = jnp.zeros_like(out_ref)
     for which, panel in zip(lists, panels):
         begin = plan_ref[which - 1] if which else 0
 
@@ -204,13 +256,15 @@
     width = panels[0].shape[-1]
     first = into is None
     operands = [plan, tiles, *panels] + ([] if first else [into])
-    return pl.pallas_call(
+    total = pltpu.VMEM((blocks_dev, block, width), jnp.float32)
+    done = pl.pallas_call(
         functools.partial(add_kernel, lists, plan.shape[0] - tile_total, slots, first),
-        out_shape=jax.ShapeDtypeStruct((blocks_dev, block, width), jnp.float32),
-        in_specs=[SMEM] + [VMEM] * (len(operands) - 1),
-        out_specs=VMEM,
+        out_shape=(total, pltpu.VMEM(tiles.shape, tiles.dtype)) if first else total,
+        in_specs=[SMEM, HBM if first else VMEM] + [VMEM] * (len(operands) - 2),
+        out_specs=(VMEM, VMEM) if first else VMEM,
+        scratch_shapes=[pltpu.SemaphoreType.DMA] if first else [],
         input_output_aliases={} if first else {len(operands) - 1: 0},
-        compiler_params=pltpu.CompilerParams(vmem_limit_bytes=24 << 20),
+        compiler_params=pltpu.CompilerParams(vmem_limit_bytes=16 << 20),
         cost_estimate=pl.CostEstimate(
             flops=20 * len(lists) * block * block * width,
             bytes_accessed=4 * blocks_dev * block * width,
@@ -218,6 +272,7 @@
         ),
         name="add",
     )(*operands)
+    return done if first else (done, tiles)
 
 
 def per_device(features, norm_gain, row_counts, tile_cols, tile_values):
@@ -231,55 +286,68 @@
     swap = functools.partial(lax.all_to_all, axis_name="rows", split_axis=0, concat_axis=0, tiled=True)
     tie = lax.optimization_barrier
     if ring:
-        lists = 3 + 2 * n
-        source, tile_cols = tie((blocks[:n], tile_cols))
+        lists = 2 + 2 * n
+        heavy_ids, mine, want, source = start_up(n, blocks_dev, tile_cols, blocks)
         first_part = swap(source)
-        want, heavy_ids, mine = find_wants(n, blocks_dev, tile_cols)
-        want = lax.psum(want, "rows")
-
-        def second_block(k, want, mine):
-            asked = jnp.clip(want[k, lax.axis_index("rows")], 0, blocks_dev - 1)
-            return jnp.where(mine[0] == 1, n + k, asked)
-
-        picked = pick_blocks(second_block, n, (want, mine), blocks, pltpu.HBM)
-        first_part, picked = tie((first_part, picked))
+        flip = lambda x, m: lax.ppermute(x, "rows", [(i, i ^ m) for i in range(n)])
+        want = [want, flip(want, 1)]
+        pair = want[0] + want[1]
+        want = [pair] + [flip(pair, m) for m in range(2, n, 2)]
+
+        def second_block(k, mine, *want):
+            me = lax.axis_index("rows")
+            asked = sum(matrix[k, me] for matrix in want)
+            return jnp.where(mine[0] == 1, n + k, jnp.clip(asked, 0, blocks_dev - 1))
+
+        picked = pick_blocks(second_block, n, (mine, *want), blocks, pltpu.VMEM, pltpu.HBM)
         second_part = swap(picked)
         order = ring_order(n)
         up = [(order[i], order[(i + 1) % n]) for i in range(n)]
         down = [(b, a) for a, b in up]
-        share = functools.partial(pick_blocks, lambda k, ids: ids[k], HEAVY, (heavy_ids,), to=pltpu.VMEM)
+        share = functools.partial(pick_blocks, lambda k, ids: ids[k], HEAVY, (heavy_ids,), at=pl.ANY, to=pltpu.VMEM)
         start = share(first_part)
         start, row_counts = tie((start, row_counts))
         plan = order_tiles(n, blocks_dev, lists, True, tile_cols, row_counts, heavy_ids)
-        add = functools.partial(add_products, plan, tile_values, blocks_dev=blocks_dev, slots=slots)
-        ahead = lax.ppermute(start, "rows", up)
-        total = add((0, 2), (blocks, start), None)
-        second_part, total = tie((second_part, total))
-        mine_back = share(second_part)
-        back = mine_back
-        ready = [(1, second_part), (3, back), (4, ahead)]
+        add = functools.partial(add_products, plan, blocks_dev=blocks_dev, slots=slots)
+
+        def hop_on(way, x):
+            return lax.ppermute(x, "rows", up if way == "up" else down)
+
+        def add_now(ready, tiles, total):
+            lists, panels = zip(*ready)
+            total, tiles = add(tiles, lists, panels, total)
+            return tiles, total
+
+        ahead = hop_on("up", start)
+        straight = hop_on("down", start)
+        sums = add_now([(0, blocks), (2, start)], tile_values, None)
+        sums = add_now([(4, ahead), (2 * n, straight)], *sums)
+        back = mine_back = share(second_part)
+        ready = [(1, second_part), (3, back)]
+        ahead = hop_on("up", ahead)
         for hop in range(1, n - 1):
-            back = lax.ppermute(back, "rows", down)
-            ahead = lax.ppermute(ahead, "rows", up)
-            total = add(tuple(g for g, _ in ready), tuple(p for _, p in ready), total)
-            ahead, total = tie((ahead, total))
-            ready = [(3 + 2 * hop, back), (4 + 2 * hop, ahead)]
-        third = HEAVY - 1
-        back = lax.ppermute(back[third:], "rows", down)
-        straight = lax.ppermute(mine_back[:third], "rows", up)
-        total = add(tuple(g for g, _ in ready), tuple(p for _, p in ready), total)
-        straight, total = tie((straight, total))
-        total = add((2 * n + 1, 2 * n + 2), (straight, back), total)
+            if hop < n - 2:
+                ready.append((4 + 2 * hop, ahead))
+            else:
+                ready.append((2 * n + 1, ahead))
+            if hop < n - 3:
+                ahead = hop_on("up", ahead)
+            elif hop == n - 3:
+                mine_back, ahead = tie((mine_back, ahead))
+                ahead = hop_on("up", mine_back)
+            back = hop_on("down", back)
+            sums = add_now(ready, *sums)
+            ready = [(3 + 2 * hop, back)]
+        _, total = add_now(ready, *sums)
     else:
-        want, heavy_ids, mine = find_wants(n, blocks_dev, tile_cols)
-        me = lax.axis_index("rows")
-        asked = swap(want[me].reshape(n, 1))[:, 0]
+        heavy_ids, _, want = find_wants(n, blocks_dev, tile_cols)
+        asked = swap(want.reshape(n, 1))[:, 0]
         plan = order_tiles(n, blocks_dev, 3, False, tile_cols, row_counts, heavy_ids)
         piece = node_dev // n
         light = swap(blocks[asked])
         scattered = swap(features.reshape(n, piece, width))[heavy_ids]
         heavy = lax.all_gather(scattered, "rows", axis=1, tiled=True).reshape(HEAVY * blocks_dev, block, width)
-        total = add_products(plan, tile_values, (0, 1, 2), (blocks, light, heavy), None, blocks_dev, slots)
+        total, _ = add_products(plan, tile_values, (0, 1, 2), (blocks, light, heavy), None, blocks_dev, slots)
     aggregate = total.reshape(node_dev, width)
     square_sum = jnp.sum(lax.all_gather(jnp.sum(aggregate * aggregate, axis=1), "feat"), axis=0)
     mean_square = square_sum / (width * lax.axis_size("feat"))

time: 146 us -> 174 us (1.19)
  waiting for transfers between devices: 28.7 us -> 72.5 us
  blocking collectives: 28 us -> 5.19 us
  starting transfers between devices: 34.8 us -> 40.6 us
  Pallas kernels: 35.9 us -> 39.3 us
    ppermute x15 -> x18, waiting for transfers between devices: 22.5 us -> 72.5 us  [the longest x14 54.3 us: hop_on(): return lax.ppermute(x, 'rows', up if way == 'up' else down)]
    psum x1 -> x0, blocking collectives: 22.8 us -> none  [per_device(): want = lax.psum(want, 'rows')]
    all_to_all x1, waiting for transfers between devices: 6.15 us -> 0.01 us  [per_device(): second_part = swap(picked)]
    ppermute x15 -> x18, starting transfers between devices: 23.9 us -> 29.7 us  [the longest x14 21.8 us: hop_on(): return lax.ppermute(x, 'rows', up if way == 'up' else down)]
    slice x3 -> x0, local copies, waits for them, and re-layouts: 2.46 us -> none  [the longest x1 2.43 us: per_device(): source, tile_cols = tie((blocks[:n], tile_cols))]
    pallas_call x9, Pallas kernels: 22.5 us -> 24.7 us  [add_products(): pl.pallas_call(functools.partial(add_kernel, lists, plan.shape[0] - tile_...]
    unnamed x26 -> x58, local copies, waits for them, and re-layouts: 13.1 us -> 13.9 us
  transfers between devices with their start and end apart: 17 -> 20, of which waited for: 11 -> 14; matrix products, arithmetic and copies ran while one was open for 0% -> 0% of each run, Pallas kernels for 24% -> 19%
where the time goes in v2:
time: 174 us
  waiting for transfers between devices  72.5 us (42%)
  starting transfers between devices  40.6 us (23%)
  Pallas kernels  39.3 us (23%)
  local copies, waits for them, and re-layouts  13.9 us (8%)
  blocking collectives  5.19 us (3%)
  other arithmetic  2.05 us (1%)
    ppermute x14, waiting for transfers between devices, hop_on(): return lax.ppermute(x, 'rows', up if way == 'up' else down)  54.3 us
    pallas_call x9, Pallas kernels, add_products(): pl.pallas_call(functools.partial(add_kernel, lists, plan.shape[0] - tile_...  24.7 us
    ppermute x14, starting transfers between devices, hop_on(): return lax.ppermute(x, 'rows', up if way == 'up' else down)  21.8 us
    ppermute x4, waiting for transfers between devices, per_device(): flip = lambda x, m: lax.ppermute(x, 'rows', [(i, i ^ m) for i in range(n)])  18.2 us
    unnamed x58, local copies, waits for them, and re-layouts  13.9 us
    ppermute x4, starting transfers between devices, per_device(): flip = lambda x, m: lax.ppermute(x, 'rows', [(i, i ^ m) for i in range(n)])  7.91 us
    all_to_all x1, starting transfers between devices, per_device(): first_part = swap(source)  7.29 us
    pallas_call x3, Pallas kernels, pick_blocks(): pl.pallas_call(functools.partial(pick_kernel, choose, count), out_shape=t...  5.38 us
  transfers between devices with their start and end apart: 20, of which 14 were waited for; matrix products, arithmetic and copies ran while one was open for 0% of the time, Pallas kernels for 19%

profile of v2, /device:TPU:0, one launch (start us, length us, event | category | flops | bytes accessed | tf_op | source)
XLA Modules:
  0.0 173.9 jit_solution(17012795543411988475)
XLA Ops:
  0.0 4.0 %head.1 = (s32[3]{0:T(128)}, s32[1]{0:T(128)}, s32[8,8]{1,0:T(8,128)}, f32[8,128,256]{2,1,0:T(8,128)}) custom-call(s32[86]{0:T(128)} %cols_ref.3, f32[16,128,256]{2,1,0:T(8,128)} %bitcast.6), custom_call_target="tpu_custom_call" | custom-call | tf_op jit(solution)/shard_map/head/pallas_call | solution.py:105
  4.0 7.3 %all-to-all-start = ((f32[8,128,256]{2,1,0:T(8,128)}), f32[8,128,256]{2,1,0:T(8,128)S(1)}, u32[]{:S(2)}, u32[]{:S(2)}) async-start(f32[8,128,256]{2,1,0:T(8,128)} %get-tuple-element.15), calls=%async_computation | async-start | bytes 2097152 | tf_op jit(solution)/shard_map/all_to_all | solution.py:291
  13.3 4.9 %collective-permute-done = s32[8,8]{1,0:T(8,128)S(1)} collective-permute-done((s32[8,8]{1,0:T(8,128)S(1)}, s32[8,8]{1,0:T(8,128)S(1)}, u32[]{:S(2)}, u32[]{:S(2)}) %collective-permute-start) | collective-permute-done | bytes 288 | tf_op jit(solution)/shard_map/ppermute | solution.py:292
  18.3 3.5 %collective-permute-start.1 = (s32[8,8]{1,0:T(8,128)S(1)}, s32[8,8]{1,0:T(8,128)S(1)}, u32[]{:S(2)}, u32[]{:S(2)}) collective-permute-start(s32[8,8]{1,0:T(8,128)S(1)} %add.22.refs_1_), channel_id=1, source_target_pairs={{0,8},{4,12},{8,0},{12,4},{16,24},{20,28},{24,16},{28,20},{1,9},{5... | collective-permute-start | bytes 776 | tf_op jit(solution)/shard_map/ppermute | solution.py:292
  24.2 4.5 %collective-permute-done.1.refs_2_ = s32[8,8]{1,0:T(8,128)S(1)} collective-permute-done((s32[8,8]{1,0:T(8,128)S(1)}, s32[8,8]{1,0:T(8,128)S(1)}, u32[]{:S(2)}, u32[]{:S(2)}) %collective-permute-start.1) | collective-permute-done | bytes 288 | tf_op jit(solution)/shard_map/ppermute | solution.py:292
  28.7 8.7 %collective-permute-done.2.refs_3_ = s32[8,8]{1,0:T(8,128)S(1)} collective-permute-done((s32[8,8]{1,0:T(8,128)S(1)}, s32[8,8]{1,0:T(8,128)S(1)}, u32[]{:S(2)}, u32[]{:S(2)}) %collective-permute-start.2) | collective-permute-done | bytes 288 | tf_op jit(solution)/shard_map/ppermute | solution.py:292
  40.9 3.6 %all-to-all-start.1 = ((f32[8,128,256]{2,1,0:T(8,128)}), f32[8,128,256]{2,1,0:T(8,128)S(1)}, u32[]{:S(2)}, u32[]{:S(2)}) async-start(f32[8,128,256]{2,1,0:T(8,128)} %pick.4), calls=%async_computation.1 | async-start | bytes 2097152 | tf_op jit(solution)/shard_map/all_to_all | solution.py:303
  49.6 20.9 %collective-permute-done.10.refs_0_ = f32[3,128,256]{2,1,0:T(8,128)S(1)} collective-permute-done((f32[3,128,256]{2,1,0:T(8,128)}, f32[3,128,256]{2,1,0:T(8,128)S(1)}, u32[]{:S(2)}, u32[]{:S(2)}) %collective-permute-start.10) | collective-permute-done | bytes 393248 | tf_op jit(solution)/shard_map/ppermute | solution.py:314
  70.5 7.0 %collective-permute-start.11 = (f32[3,128,256]{2,1,0:T(8,128)S(1)}, f32[3,128,256]{2,1,0:T(8,128)S(1)}, u32[]{:S(2)}, u32[]{:S(2)}) collective-permute-start(f32[3,128,256]{2,1,0:T(8,128)S(1)} %collective-permute-done.10.refs_0_), channel_id=1, source_target_pairs={{0,8},{8,16},{16,24},{24,28},{28,20},{20,12},{12,4},{4,0},{1,9},{9... | collective-permute-start | bytes 1179656 | tf_op jit(solution)/shard_map/ppermute | solution.py:314
  78.7 7.4 %collective-permute-done.11.refs_2_ = f32[3,128,256]{2,1,0:T(8,128)S(1)} collective-permute-done((f32[3,128,256]{2,1,0:T(8,128)S(1)}, f32[3,128,256]{2,1,0:T(8,128)S(1)}, u32[]{:S(2)}, u32[]{:S(2)}) %collective-permute-start.11) | collective-permute-done | bytes 393248 | tf_op jit(solution)/shard_map/ppermute | solution.py:314
  86.1 2.5 %collective-permute-start.12 = (f32[3,128,256]{2,1,0:T(8,128)S(1)}, f32[3,128,256]{2,1,0:T(8,128)S(1)}, u32[]{:S(2)}, u32[]{:S(2)}) collective-permute-start(f32[3,128,256]{2,1,0:T(8,128)S(1)} %collective-permute-done.11.refs_2_), channel_id=1, source_target_pairs={{0,8},{8,16},{16,24},{24,28},{28,20},{20,12},{12,4},{4,0},{1,9},{9... | collective-permute-start | bytes 1179656 | tf_op jit(solution)/shard_map/ppermute | solution.py:314
  90.9 6.1 %collective-permute-done.12.refs_1_ = f32[3,128,256]{2,1,0:T(8,128)S(1)} collective-permute-done((f32[3,128,256]{2,1,0:T(8,128)S(1)}, f32[3,128,256]{2,1,0:T(8,128)S(1)}, u32[]{:S(2)}, u32[]{:S(2)}) %collective-permute-start.12) | collective-permute-done | bytes 393248 | tf_op jit(solution)/shard_map/ppermute | solution.py:314
  101.3 4.9 %collective-permute-done.13.refs_1_ = f32[3,128,256]{2,1,0:T(8,128)S(1)} collective-permute-done((f32[3,128,256]{2,1,0:T(8,128)S(1)}, f32[3,128,256]{2,1,0:T(8,128)S(1)}, u32[]{:S(2)}, u32[]{:S(2)}) %collective-permute-start.13) | collective-permute-done | bytes 393248 | tf_op jit(solution)/shard_map/ppermute | solution.py:314
  111.0 4.5 %collective-permute-done.14.refs_1_ = f32[3,128,256]{2,1,0:T(8,128)S(1)} collective-permute-done((f32[3,128,256]{2,1,0:T(8,128)S(1)}, f32[3,128,256]{2,1,0:T(8,128)S(1)}, u32[]{:S(2)}, u32[]{:S(2)}) %collective-permute-start.14) | collective-permute-done | bytes 393248 | tf_op jit(solution)/shard_map/ppermute | solution.py:314
  120.5 3.5 %collective-permute-done.15.refs_1_ = f32[3,128,256]{2,1,0:T(8,128)S(1)} collective-permute-done((f32[3,128,256]{2,1,0:T(8,128)S(1)}, f32[3,128,256]{2,1,0:T(8,128)S(1)}, u32[]{:S(2)}, u32[]{:S(2)}) %collective-permute-start.15) | collective-permute-done | bytes 393248 | tf_op jit(solution)/shard_map/ppermute | solution.py:314
  127.0 4.0 %collective-permute-done.8.refs_0_ = f32[3,128,256]{2,1,0:T(8,128)} collective-permute-done((f32[3,128,256]{2,1,0:T(8,128)S(1)}, f32[3,128,256]{2,1,0:T(8,128)}, u32[]{:S(2)}, u32[]{:S(2)}) %collective-permute-start.8) | collective-permute-done | bytes 393248 | tf_op jit(solution)/shard_map/ppermute | solution.py:314
  131.6 5.2 %order.1.plan_ref = s32[104]{0:T(128)} custom-call(s32[86]{0:T(128)} %cols_ref.3, s32[1,16]{1,0:T(1,128)} %counts_ref, s32[3]{0:T(128)} %get-tuple-element.14.refs_0_.heavy_ref), custom_call_target="tpu_custom_call" | custom-call | tf_op jit(solution)/shard_map/order/pallas_call | solution.py:184
  138.4 2.6 %copy-done.2 = f32[86,128,128]{2,1,0:T(8,128)S(1)} copy-done((f32[86,128,128]{2,1,0:T(8,128)S(1)}, f32[86,128,128]{2,1,0:T(8,128)}, u32[]{:S(2)}) %copy-start.2) | copy-done | bytes 5636120
  141.6 6.3 %add.27 = (f32[16,128,256]{2,1,0:T(8,128)S(1)}, f32[86,128,128]{2,1,0:T(8,128)S(1)}) custom-call(s32[104]{0:T(128)S(1)} %copy-done.25, f32[86,128,128]{2,1,0:T(8,128)S(1)} %copy-done.2, f32[16,128,256]{2,1,0:T(8,128)S(1)} %bitcast.8, f32[3,128,256]{2,1,0:T(8,128)} %pick.3.refs_1_), custom_call_target="tpu_custom_call" | custom-call | flops 167772160 | bytes 2097152 | tf_op jit(solution)/shard_map/add/pallas_call | solution.py:260
  147.9 2.6 %add.28.refs_3_ = f32[16,128,256]{2,1,0:T(8,128)S(1)} custom-call(s32[104]{0:T(128)S(1)} %copy-done.25, f32[86,128,128]{2,1,0:T(8,128)S(1)} %get-tuple-element.18.tiles_ref, f32[3,128,256]{2,1,0:T(8,128)S(1)} %copy-done.8, f32[3,128,256]{2,1,0:T(8,128)} %collective-permute-done.17.refs_1_, ...), custom_call_target="tpu_custom_call", output_to_operand_aliasing={{}: (4, {})} | custom-call | flops 167772160 | bytes 2097152 | tf_op jit(solution)/shard_map/add/pallas_call | solution.py:260
  150.6 2.7 %add.29.refs_2_ = f32[16,128,256]{2,1,0:T(8,128)S(1)} custom-call(s32[104]{0:T(128)S(1)} %copy-done.25, f32[86,128,128]{2,1,0:T(8,128)S(1)} %get-tuple-element.18.tiles_ref, f32[8,128,256]{2,1,0:T(8,128)S(1)} %all-to-all-done.1.refs_1_.refs_0_, f32[3,128,256]{2,1,0:T(8,128)S(1)} %pick.5.refs_1_, ...), custom_call_target="tpu_custom_call", output_to_operand_aliasing={{}: (5, {})} | custom-call | flops 251658240 | bytes 2097152 | tf_op jit(solution)/shard_map/add/pallas_call | solution.py:260
  153.4 2.7 %add.30.refs_2_ = f32[16,128,256]{2,1,0:T(8,128)S(1)} custom-call(s32[104]{0:T(128)S(1)} %copy-done.25, f32[86,128,128]{2,1,0:T(8,128)S(1)} %get-tuple-element.18.tiles_ref, f32[3,128,256]{2,1,0:T(8,128)S(1)} %copy-done.10, f32[3,128,256]{2,1,0:T(8,128)S(1)} %copy-done.12, f32[16,128,256]{2,1,0:T(8,128)S(1)} %add.29.refs_2_), custom_call_target="tpu_custom_call", output_to_operand_aliasing={{}: (4, {})} | custom-call | flops 167772160 | bytes 2097152 | tf_op jit(solution)/shard_map/add/pallas_call | solution.py:260
  162.5 2.5 %add.34.refs_1_ = f32[16,128,256]{2,1,0:T(8,128)S(1)} custom-call(s32[104]{0:T(128)S(1)} %copy-done.25, f32[86,128,128]{2,1,0:T(8,128)S(1)} %get-tuple-element.18.tiles_ref, f32[3,128,256]{2,1,0:T(8,128)} %collective-permute-done.8.refs_0_, f32[3,128,256]{2,1,0:T(8,128)} %collective-permute-done.16.refs_1_, ...), custom_call_target="tpu_custom_call", output_to_operand_aliasing={{}: (4, {})} | custom-call | flops 167772160 | bytes 2097152 | tf_op jit(solution)/shard_map/add/pallas_call | solution.py:260
  167.0 5.2 %all-gather = f32[4,1,2048]{2,1,0:T(1,128)S(1)} all-gather(f32[1,1,2048]{2,1,0:T(1,128)S(1)} %bitcast.9), channel_id=1, replica_groups=mesh['rows'=8,'feat'=4] {'feat'}, dimensions={0}, use_global_device_ids=true | all-gather | bytes 40960 | tf_op jit(solution)/shard_map/all_gather | solution.py:352
  (94 shorter events, 46.2 us)
Async XLA Ops:
  0.0 37.4 %copy-start = (f32[2048,256]{1,0:T(8,128)S(1)}, f32[2048,256]{1,0:T(8,128)}, u32[]{:S(2)}) copy-start(f32[2048,256]{1,0:T(8,128)} %param.5) | copy-start | bytes 6291460
  4.0 7.3 %copy-start.27 = (s32[8,8]{1,0:T(8,128)S(1)}, s32[8,8]{1,0:T(8,128)}, u32[]{:S(2)}) copy-start(s32[8,8]{1,0:T(8,128)} %get-tuple-element.20) | copy-start | bytes 772
  4.0 35.9 %all-to-all-start = ((f32[8,128,256]{2,1,0:T(8,128)}), f32[8,128,256]{2,1,0:T(8,128)S(1)}, u32[]{:S(2)}, u32[]{:S(2)}) async-start(f32[8,128,256]{2,1,0:T(8,128)} %get-tuple-element.15), calls=%async_computation | async-start | bytes 2097152 | tf_op jit(solution)/shard_map/all_to_all | solution.py:291
  11.3 6.9 %collective-permute-start = (s32[8,8]{1,0:T(8,128)S(1)}, s32[8,8]{1,0:T(8,128)S(1)}, u32[]{:S(2)}, u32[]{:S(2)}) collective-permute-start(s32[8,8]{1,0:T(8,128)S(1)} %copy-done.27), channel_id=1, source_target_pairs={{0,4},{4,0},{8,12},{12,8},{16,20},{20,16},{24,28},{28,24},{1,5},{5... | collective-permute-start | bytes 776 | tf_op jit(solution)/shard_map/ppermute | solution.py:292
  18.3 10.4 %collective-permute-start.1 = (s32[8,8]{1,0:T(8,128)S(1)}, s32[8,8]{1,0:T(8,128)S(1)}, u32[]{:S(2)}, u32[]{:S(2)}) collective-permute-start(s32[8,8]{1,0:T(8,128)S(1)} %add.22.refs_1_), channel_id=1, source_target_pairs={{0,8},{4,12},{8,0},{12,4},{16,24},{20,28},{24,16},{28,20},{1,9},{5... | collective-permute-start | bytes 776 | tf_op jit(solution)/shard_map/ppermute | solution.py:292
  21.8 15.6 %collective-permute-start.2 = (s32[8,8]{1,0:T(8,128)S(1)}, s32[8,8]{1,0:T(8,128)S(1)}, u32[]{:S(2)}, u32[]{:S(2)}) collective-permute-start(s32[8,8]{1,0:T(8,128)S(1)} %add.22.refs_1_), channel_id=1, source_target_pairs={{0,16},{4,20},{8,24},{12,28},{16,0},{20,4},{24,8},{28,12},{1,17},{... | collective-permute-start | bytes 776 | tf_op jit(solution)/shard_map/ppermute | solution.py:292
  23.9 13.5 %collective-permute-start.3 = (s32[8,8]{1,0:T(8,128)S(1)}, s32[8,8]{1,0:T(8,128)S(1)}, u32[]{:S(2)}, u32[]{:S(2)}) collective-permute-start(s32[8,8]{1,0:T(8,128)S(1)} %add.22.refs_1_), channel_id=1, source_target_pairs={{0,24},{4,28},{8,16},{12,20},{16,8},{20,12},{24,0},{28,4},{1,25},{... | collective-permute-start | bytes 776 | tf_op jit(solution)/shard_map/ppermute | solution.py:292
  37.4 7.1 %copy-start.26 = (s32[3]{0:T(128)S(1)}, s32[3]{0:T(128)}, u32[]{:S(2)}) copy-start(s32[3]{0:T(128)} %get-tuple-element.14.refs_0_.heavy_ref) | copy-start | bytes 40
  40.9 36.7 %all-to-all-start.1 = ((f32[8,128,256]{2,1,0:T(8,128)}), f32[8,128,256]{2,1,0:T(8,128)S(1)}, u32[]{:S(2)}, u32[]{:S(2)}) async-start(f32[8,128,256]{2,1,0:T(8,128)} %pick.4), calls=%async_computation.1 | async-start | bytes 2097152 | tf_op jit(solution)/shard_map/all_to_all | solution.py:303
  47.5 23.0 %collective-permute-start.10 = (f32[3,128,256]{2,1,0:T(8,128)}, f32[3,128,256]{2,1,0:T(8,128)S(1)}, u32[]{:S(2)}, u32[]{:S(2)}) collective-permute-start(f32[3,128,256]{2,1,0:T(8,128)} %pick.3.refs_1_), channel_id=1, source_target_pairs={{0,8},{8,16},{16,24},{24,28},{28,20},{20,12},{12,4},{4,0},{1,9},{9... | collective-permute-start | bytes 1179656 | tf_op jit(solution)/shard_map/ppermute | solution.py:314
  70.5 61.0 %copy-start.7 = (f32[3,128,256]{2,1,0:T(8,128)}, f32[3,128,256]{2,1,0:T(8,128)S(1)}, u32[]{:S(2)}) copy-start(f32[3,128,256]{2,1,0:T(8,128)S(1)} %collective-permute-done.10.refs_0_) | copy-start | bytes 1179652
  70.5 15.6 %collective-permute-start.11 = (f32[3,128,256]{2,1,0:T(8,128)S(1)}, f32[3,128,256]{2,1,0:T(8,128)S(1)}, u32[]{:S(2)}, u32[]{:S(2)}) collective-permute-start(f32[3,128,256]{2,1,0:T(8,128)S(1)} %collective-permute-done.10.refs_0_), channel_id=1, source_target_pairs={{0,8},{8,16},{16,24},{24,28},{28,20},{20,12},{12,4},{4,0},{1,9},{9... | collective-permute-start | bytes 1179656 | tf_op jit(solution)/shard_map/ppermute | solution.py:314
  78.7 11.4 %collective-permute-start.4 = (f32[3,128,256]{2,1,0:T(8,128)S(1)}, f32[3,128,256]{2,1,0:T(8,128)S(1)}, u32[]{:S(2)}, u32[]{:S(2)}) collective-permute-start(f32[3,128,256]{2,1,0:T(8,128)S(1)} %pick.5.refs_1_), channel_id=1, source_target_pairs={{8,0},{16,8},{24,16},{28,24},{20,28},{12,20},{4,12},{0,4},{9,1},{1... | collective-permute-start | bytes 1179656 | tf_op jit(solution)/shard_map/ppermute | solution.py:314
  86.1 10.8 %collective-permute-start.12 = (f32[3,128,256]{2,1,0:T(8,128)S(1)}, f32[3,128,256]{2,1,0:T(8,128)S(1)}, u32[]{:S(2)}, u32[]{:S(2)}) collective-permute-start(f32[3,128,256]{2,1,0:T(8,128)S(1)} %collective-permute-done.11.refs_2_), channel_id=1, source_target_pairs={{0,8},{8,16},{16,24},{24,28},{28,20},{20,12},{12,4},{4,0},{1,9},{9... | collective-permute-start | bytes 1179656 | tf_op jit(solution)/shard_map/ppermute | solution.py:314
  90.1 10.2 %collective-permute-start.5 = (f32[3,128,256]{2,1,0:T(8,128)S(1)}, f32[3,128,256]{2,1,0:T(8,128)S(1)}, u32[]{:S(2)}, u32[]{:S(2)}) collective-permute-start(f32[3,128,256]{2,1,0:T(8,128)S(1)} %collective-permute-done.4.refs_0_), channel_id=1, source_target_pairs={{8,0},{16,8},{24,16},{28,24},{20,28},{12,20},{4,12},{0,4},{9,1},{1... | collective-permute-start | bytes 1179656 | tf_op jit(solution)/shard_map/ppermute | solution.py:314
  97.0 9.2 %collective-permute-start.13 = (f32[3,128,256]{2,1,0:T(8,128)S(1)}, f32[3,128,256]{2,1,0:T(8,128)S(1)}, u32[]{:S(2)}, u32[]{:S(2)}) collective-permute-start(f32[3,128,256]{2,1,0:T(8,128)S(1)} %collective-permute-done.12.refs_1_), channel_id=1, source_target_pairs={{0,8},{8,16},{16,24},{24,28},{28,20},{20,12},{12,4},{4,0},{1,9},{9... | collective-permute-start | bytes 1179656 | tf_op jit(solution)/shard_map/ppermute | solution.py:314
  100.3 9.3 %collective-permute-start.6 = (f32[3,128,256]{2,1,0:T(8,128)S(1)}, f32[3,128,256]{2,1,0:T(8,128)S(1)}, u32[]{:S(2)}, u32[]{:S(2)}) collective-permute-start(f32[3,128,256]{2,1,0:T(8,128)S(1)} %collective-permute-done.5.refs_0_), channel_id=1, source_target_pairs={{8,0},{16,8},{24,16},{28,24},{20,28},{12,20},{4,12},{0,4},{9,1},{1... | collective-permute-start | bytes 1179656 | tf_op jit(solution)/shard_map/ppermute | solution.py:314
  106.2 9.2 %collective-permute-start.14 = (f32[3,128,256]{2,1,0:T(8,128)S(1)}, f32[3,128,256]{2,1,0:T(8,128)S(1)}, u32[]{:S(2)}, u32[]{:S(2)}) collective-permute-start(f32[3,128,256]{2,1,0:T(8,128)S(1)} %collective-permute-done.13.refs_1_), channel_id=1, source_target_pairs={{0,8},{8,16},{16,24},{24,28},{28,20},{20,12},{12,4},{4,0},{1,9},{9... | collective-permute-start | bytes 1179656 | tf_op jit(solution)/shard_map/ppermute | solution.py:314
  109.6 9.3 %collective-permute-start.7 = (f32[3,128,256]{2,1,0:T(8,128)S(1)}, f32[3,128,256]{2,1,0:T(8,128)S(1)}, u32[]{:S(2)}, u32[]{:S(2)}) collective-permute-start(f32[3,128,256]{2,1,0:T(8,128)S(1)} %collective-permute-done.6.refs_0_), channel_id=1, source_target_pairs={{8,0},{16,8},{24,16},{28,24},{20,28},{12,20},{4,12},{0,4},{9,1},{1... | collective-permute-start | bytes 1179656 | tf_op jit(solution)/shard_map/ppermute | solution.py:314
  115.5 8.6 %collective-permute-start.15 = (f32[3,128,256]{2,1,0:T(8,128)S(1)}, f32[3,128,256]{2,1,0:T(8,128)S(1)}, u32[]{:S(2)}, u32[]{:S(2)}) collective-permute-start(f32[3,128,256]{2,1,0:T(8,128)S(1)} %collective-permute-done.14.refs_1_), channel_id=1, source_target_pairs={{0,8},{8,16},{16,24},{24,28},{28,20},{20,12},{12,4},{4,0},{1,9},{9... | collective-permute-start | bytes 1179656 | tf_op jit(solution)/shard_map/ppermute | solution.py:314
  118.9 12.1 %collective-permute-start.8 = (f32[3,128,256]{2,1,0:T(8,128)S(1)}, f32[3,128,256]{2,1,0:T(8,128)}, u32[]{:S(2)}, u32[]{:S(2)}) collective-permute-start(f32[3,128,256]{2,1,0:T(8,128)S(1)} %collective-permute-done.7.refs_0_), channel_id=1, source_target_pairs={{8,0},{16,8},{24,16},{28,24},{20,28},{12,20},{4,12},{0,4},{9,1},{1... | collective-permute-start | bytes 1179656 | tf_op jit(solution)/shard_map/ppermute | solution.py:314
  120.2 27.7 %collective-permute-start.17 = (f32[3,128,256]{2,1,0:T(8,128)}, f32[3,128,256]{2,1,0:T(8,128)}, u32[]{:S(2)}, u32[]{:S(2)}) collective-permute-start(f32[3,128,256]{2,1,0:T(8,128)} %pick.3.refs_1_), channel_id=1, source_target_pairs={{8,0},{16,8},{24,16},{28,24},{20,28},{12,20},{4,12},{0,4},{9,1},{1... | collective-permute-start | bytes 1179656 | tf_op jit(solution)/shard_map/ppermute | solution.py:314
  124.8 37.6 %collective-permute-start.16 = (f32[3,128,256]{2,1,0:T(8,128)S(1)}, f32[3,128,256]{2,1,0:T(8,128)}, u32[]{:S(2)}, u32[]{:S(2)}) collective-permute-start(f32[3,128,256]{2,1,0:T(8,128)S(1)} %pick.5.refs_1_), channel_id=1, source_target_pairs={{0,8},{8,16},{16,24},{24,28},{28,20},{20,12},{12,4},{4,0},{1,9},{9... | collective-permute-start | bytes 1179656 | tf_op jit(solution)/shard_map/ppermute | solution.py:314
  131.0 34.0 %collective-permute-start.9 = (f32[3,128,256]{2,1,0:T(8,128)}, f32[3,128,256]{2,1,0:T(8,128)}, u32[]{:S(2)}, u32[]{:S(2)}) collective-permute-start(f32[3,128,256]{2,1,0:T(8,128)} %collective-permute-done.8.refs_0_), channel_id=1, source_target_pairs={{8,0},{16,8},{24,16},{28,24},{20,28},{12,20},{4,12},{0,4},{9,1},{1... | collective-permute-start | bytes 1179656 | tf_op jit(solution)/shard_map/ppermute | solution.py:314
  (25 other events, 48.1 us)

commit v3 on v2

--- a/solution.py
+++ b/solution.py
@@ -11,6 +11,7 @@
 HEAVY = 3
 SMEM = pl.BlockSpec(memory_space=pltpu.SMEM)
 HBM = pl.BlockSpec(memory_space=pltpu.HBM)
+ANY = pl.BlockSpec(memory_space=pl.ANY)
 VMEM = pl.BlockSpec(memory_space=pltpu.VMEM)
 
 
@@ -76,51 +77,74 @@
     )(tile_cols)
 
 
-def head_kernel(
-    n, blocks_dev, tile_total, cols_ref, from_ref,
-    heavy_ref, mine_ref, want_ref, half_ref,
-    seen_ref, last_ref, buf_ref, in_sem, out_sem,
-):
-    ins = [pltpu.make_async_copy(from_ref.at[k], buf_ref.at[k], in_sem.at[k]) for k in range(n)]
-    outs = [pltpu.make_async_copy(buf_ref.at[k], half_ref.at[k], out_sem.at[k]) for k in range(n)]
-    for copy in ins:
+def head_kernel(n, blocks_dev, tile_total, cols_ref, from_ref, heavy_ref, mine_ref, want_ref, *refs):
+    letters, (seen_ref, last_ref, sem_ref) = refs[: n - 1], refs[n - 1:]
+    copies = [pltpu.make_async_copy(from_ref.at[m], letters[m - 1], sem_ref.at[m - 1]) for m in range(1, n)]
+    for copy in copies:
         copy.start()
     me = lax.axis_index("rows")
     for o in range(n):
         for p in range(n):
             want_ref[o, p] = 0
-    for copy, onward in zip(ins, outs):
-        copy.wait()
-        onward.start()
     find_heavy(n, blocks_dev, tile_total, cols_ref, heavy_ref, mine_ref, seen_ref, last_ref)
     for p in range(n):
         want_ref[me, p] = last_ref[p]
-    for copy in outs:
+    for copy in copies:
         copy.wait()
 
 
 def start_up(n, blocks_dev, tile_cols, blocks):
     tile_total = tile_cols.shape[0]
-    shape = (n, *blocks.shape[1:])
-    return pl.pallas_call(
+    letter = pltpu.VMEM(blocks.shape[1:], jnp.float32)
+    heavy_ids, mine, want, *letters = pl.pallas_call(
         functools.partial(head_kernel, n, blocks_dev, tile_total),
         out_shape=(
             jax.ShapeDtypeStruct((HEAVY,), jnp.int32),
             jax.ShapeDtypeStruct((1,), jnp.int32),
             jax.ShapeDtypeStruct((n, n), jnp.int32),
-            pltpu.HBM(shape, jnp.float32),
+            *[letter] * (n - 1),
         ),
         in_specs=[SMEM, HBM],
-        out_specs=(SMEM, SMEM, SMEM, HBM),
+        out_specs=(SMEM, SMEM, SMEM, *[VMEM] * (n - 1)),
         scratch_shapes=[
             pltpu.SMEM((n,), jnp.int32),
             pltpu.SMEM((n,), jnp.int32),
-            pltpu.VMEM(shape, jnp.float32),
-            pltpu.SemaphoreType.DMA((n,)),
-            pltpu.SemaphoreType.DMA((n,)),
+            pltpu.SemaphoreType.DMA((n - 1,)),
         ],
+        compiler_params=pltpu.CompilerParams(vmem_limit_bytes=58 << 20),
         name="head",
-    )(tile_cols, blocks)
+    )(tile_cols, pltpu.with_memory_space_constraint(blocks, pltpu.HBM))
+    return heavy_ids, mine, want, letters
+
+
+def share_kernel(n, home, heavy_ref, from_ref, *refs):
+    got, (out_ref, sem_ref) = refs[: n - 1], refs[n - 1:]
+    me = lax.axis_index("rows")
+    for k in range(HEAVY):
+        away = heavy_ref[k] ^ me
+        for m in range(n):
+            source = from_ref.at[home] if m == 0 else got[m - 1]
+
+            @pl.when(away == m)
+            def _(source=source, k=k):
+                pltpu.make_async_copy(source, out_ref.at[k], sem_ref.at[k]).start()
+
+    for k in range(HEAVY):
+        pltpu.make_async_copy(from_ref.at[home], out_ref.at[k], sem_ref.at[k]).wait()
+
+
+def take_share(n, home, heavy_ids, blocks, got):
+    _, block, width = blocks.shape
+    return pl.pallas_call(
+        functools.partial(share_kernel, n, home),
+        out_shape=jax.ShapeDtypeStruct((HEAVY, block, width), jnp.float32),
+        in_specs=[SMEM, ANY] + [ANY] * (n - 1),
+        out_specs=VMEM,
+        scratch_shapes=[pltpu.SemaphoreType.DMA((HEAVY,))],
+        compiler_params=pltpu.CompilerParams(vmem_limit_bytes=8 << 20),
+        cost_estimate=pl.CostEstimate(flops=0, bytes_accessed=8 * HEAVY * block * width, transcendentals=0),
+        name="share",
+    )(heavy_ids, blocks, *got)
 
 
 def order_kernel(
@@ -144,7 +168,7 @@
                 heavy_at = jnp.where(owner == heavy_ref[k], k, heavy_at)
             if ring:
                 half = local // n
-                there = ring_place(local % n, n)
+                there = ring_place(jnp.where(half == 0, owner ^ (local % n), local % n), n)
                 hops = jnp.where(half == 0, here - there, there - here)
                 hops = jnp.where(hops < 0, hops + n, hops)
                 heavy_list, heavy_slot = 2 + 2 * hops + half, heavy_at
@@ -287,8 +311,10 @@
     tie = lax.optimization_barrier
     if ring:
         lists = 2 + 2 * n
-        heavy_ids, mine, want, source = start_up(n, blocks_dev, tile_cols, blocks)
-        first_part = swap(source)
+        heavy_ids, mine, want, letters = start_up(n, blocks_dev, tile_cols, blocks)
+        got = {}
+        for m in (*range(n // 2, n), *range(1, n // 2)):
+            got[m] = lax.ppermute(letters[m - 1], "rows", [(i, i ^ m) for i in range(n)])
         flip = lambda x, m: lax.ppermute(x, "rows", [(i, i ^ m) for i in range(n)])
         want = [want, flip(want, 1)]
         pair = want[0] + want[1]
@@ -305,7 +331,7 @@
         up = [(order[i], order[(i + 1) % n]) for i in range(n)]
         down = [(b, a) for a, b in up]
         share = functools.partial(pick_blocks, lambda k, ids: ids[k], HEAVY, (heavy_ids,), at=pl.ANY, to=pltpu.VMEM)
-        start = share(first_part)
+        start = take_share(n, 0, heavy_ids, blocks, [got[m] for m in range(1, n)])
         start, row_counts = tie((start, row_counts))
         plan = order_tiles(n, blocks_dev, lists, True, tile_cols, row_counts, heavy_ids)
         add = functools.partial(add_products, plan, blocks_dev=blocks_dev, slots=slots)

time: 174 us -> 181 us (1.040)
  starting transfers between devices: 40.6 us -> 49.3 us
    ppermute x0 -> x7, waiting for transfers between devices: none -> 27.2 us  [per_device(): lax.ppermute(letters[m - 1], 'rows', [(i, i ^ m) for i in range(n)])]
    ppermute x0 -> x7, starting transfers between devices: none -> 15.8 us  [per_device(): lax.ppermute(letters[m - 1], 'rows', [(i, i ^ m) for i in range(n)])]
    ppermute x14, waiting for transfers between devices: 54.3 us -> 39.3 us  [hop_on(): return lax.ppermute(x, 'rows', up if way == 'up' else down)]
    ppermute x4, waiting for transfers between devices: 18.2 us -> 5.74 us  [per_device(): flip = lambda x, m: lax.ppermute(x, 'rows', [(i, i ^ m) for i in range(n)])]
    all_to_all x1 -> x0, starting transfers between devices: 7.29 us -> none  [per_device(): first_part = swap(source)]
    pallas_call x0 -> x1, Pallas kernels: none -> 1.95 us  [take_share(): pl.pallas_call(functools.partial(share_kernel, n, home), out_shape=jax.Sh...]
    pallas_call x3 -> x2, Pallas kernels: 5.38 us -> 3.47 us  [pick_blocks(): pl.pallas_call(functools.partial(pick_kernel, choose, count), out_shape=t...]
    unnamed x58 -> x60, local copies, waits for them, and re-layouts: 13.9 us -> 12.3 us
  transfers between devices with their start and end apart: 20 -> 26, of which waited for: 14 -> 17; matrix products, arithmetic and copies ran while one was open for 0% -> 0% of each run, Pallas kernels for 19% -> 17%
where the time goes in v3:
time: 181 us
  waiting for transfers between devices  72.3 us (40%)
  starting transfers between devices  49.3 us (27%)
  Pallas kernels  38.4 us (21%)
  local copies, waits for them, and re-layouts  12.3 us (7%)
  blocking collectives  5.19 us (3%)
  other arithmetic  2.73 us (2%)
    ppermute x14, waiting for transfers between devices, hop_on(): return lax.ppermute(x, 'rows', up if way == 'up' else down)  39.3 us
    ppermute x7, waiting for transfers between devices, per_device(): lax.ppermute(letters[m - 1], 'rows', [(i, i ^ m) for i in range(n)])  27.2 us
    pallas_call x9, Pallas kernels, add_products(): pl.pallas_call(functools.partial(add_kernel, lists, plan.shape[0] - tile_...  24.7 us
    ppermute x14, starting transfers between devices, hop_on(): return lax.ppermute(x, 'rows', up if way == 'up' else down)  21.6 us
    ppermute x7, starting transfers between devices, per_device(): lax.ppermute(letters[m - 1], 'rows', [(i, i ^ m) for i in range(n)])  15.8 us
    unnamed x60, local copies, waits for them, and re-layouts  12.3 us
    ppermute x4, starting transfers between devices, per_device(): flip = lambda x, m: lax.ppermute(x, 'rows', [(i, i ^ m) for i in range(n)])  7.67 us
    ppermute x4, waiting for transfers between devices, per_device(): flip = lambda x, m: lax.ppermute(x, 'rows', [(i, i ^ m) for i in range(n)])  5.74 us
  transfers between devices with their start and end apart: 26, of which 17 were waited for; matrix products, arithmetic and copies ran while one was open for 0% of the time, Pallas kernels for 17%

profile of v3, /device:TPU:0, one launch (start us, length us, event | category | flops | bytes accessed | tf_op | source)
XLA Modules:
  0.0 180.7 jit_solution(16344273646304860121)
XLA Ops:
  0.0 3.0 %head.1 = (s32[3]{0:T(128)}, s32[1]{0:T(128)}, s32[8,8]{1,0:T(8,128)}, f32[128,256]{1,0:T(8,128)S(1)}, f32[128,256]{1,0:T(8,128)S(1)}, /*index=5*/f32[128,256]{1...) custom-call(s32[86]{0:T(128)} %cols_ref.3, ...), custom_call_target="tpu_custom_call" | custom-call | tf_op jit(solution)/shard_map/head/pallas_call | solution.py:99
  3.6 3.0 %collective-permute-start.7 = (s32[8,8]{1,0:T(8,128)}, s32[8,8]{1,0:T(8,128)S(1)}, u32[]{:S(2)}, u32[]{:S(2)}) collective-permute-start(s32[8,8]{1,0:T(8,128)} %get-tuple-element.32), channel_id=1, source_target_pairs={{0,4},{4,0},{8,12},{12,8},{16,20},{20,16},{24,28},{28,24},{1,5},{5... | collective-permute-start | bytes 776 | tf_op jit(solution)/shard_map/ppermute | solution.py:318
  9.1 4.1 %collective-permute-start.10 = (s32[8,8]{1,0:T(8,128)S(1)}, s32[8,8]{1,0:T(8,128)S(1)}, u32[]{:S(2)}, u32[]{:S(2)}) collective-permute-start(s32[8,8]{1,0:T(8,128)S(1)} %add.22.refs_1_), channel_id=1, source_target_pairs={{0,24},{4,28},{8,16},{12,20},{16,8},{20,12},{24,0},{28,4},{1,25},{... | collective-permute-start | bytes 776 | tf_op jit(solution)/shard_map/ppermute | solution.py:318
  20.2 4.2 %all-to-all-start = ((f32[8,128,256]{2,1,0:T(8,128)}), f32[8,128,256]{2,1,0:T(8,128)S(1)}, u32[]{:S(2)}, u32[]{:S(2)}) async-start(f32[8,128,256]{2,1,0:T(8,128)} %pick.2), calls=%async_computation | async-start | bytes 2097152 | tf_op jit(solution)/shard_map/all_to_all | solution.py:329
  27.9 2.9 %collective-permute-start.3 = (f32[128,256]{1,0:T(8,128)}, f32[128,256]{1,0:T(8,128)S(1)}, u32[]{:S(2)}, u32[]{:S(2)}) collective-permute-start(f32[128,256]{1,0:T(8,128)} %copy-done.25), channel_id=1, source_target_pairs={{0,16},{4,20},{8,24},{12,28},{16,0},{20,4},{24,8},{28,12},{1,17},{... | collective-permute-start | bytes 393224 | tf_op jit(solution)/shard_map/ppermute | solution.py:317
  34.6 3.3 %collective-permute-start.5 = (f32[128,256]{1,0:T(8,128)S(1)}, f32[128,256]{1,0:T(8,128)S(1)}, u32[]{:S(2)}, u32[]{:S(2)}) collective-permute-start(f32[128,256]{1,0:T(8,128)S(1)} %get-tuple-element.26), channel_id=1, source_target_pairs={{0,24},{4,28},{8,16},{12,20},{16,8},{20,12},{24,0},{28,4},{1,25},{... | collective-permute-start | bytes 393224 | tf_op jit(solution)/shard_map/ppermute | solution.py:317
  37.9 7.7 %collective-permute-done.1.refs_1_ = f32[128,256]{1,0:T(8,128)S(1)} collective-permute-done((f32[128,256]{1,0:T(8,128)}, f32[128,256]{1,0:T(8,128)S(1)}, u32[]{:S(2)}, u32[]{:S(2)}) %collective-permute-start.1) | collective-permute-done | bytes 131104 | tf_op jit(solution)/shard_map/ppermute | solution.py:317
  45.6 4.6 %collective-permute-start.6 = (f32[128,256]{1,0:T(8,128)S(1)}, f32[128,256]{1,0:T(8,128)S(1)}, u32[]{:S(2)}, u32[]{:S(2)}) collective-permute-start(f32[128,256]{1,0:T(8,128)S(1)} %get-tuple-element.27), channel_id=1, source_target_pairs={{0,28},{4,24},{8,20},{12,16},{16,12},{20,8},{24,4},{28,0},{1,29},{... | collective-permute-start | bytes 393224 | tf_op jit(solution)/shard_map/ppermute | solution.py:317
  50.2 13.9 %collective-permute-done.3.refs_3_ = f32[128,256]{1,0:T(8,128)S(1)} collective-permute-done((f32[128,256]{1,0:T(8,128)}, f32[128,256]{1,0:T(8,128)S(1)}, u32[]{:S(2)}, u32[]{:S(2)}) %collective-permute-start.3) | collective-permute-done | bytes 131104 | tf_op jit(solution)/shard_map/ppermute | solution.py:317
  64.2 3.3 %collective-permute-done.4.refs_4_ = f32[128,256]{1,0:T(8,128)S(1)} collective-permute-done((f32[128,256]{1,0:T(8,128)S(1)}, f32[128,256]{1,0:T(8,128)S(1)}, u32[]{:S(2)}, u32[]{:S(2)}) %collective-permute-start.4) | collective-permute-done | bytes 131104 | tf_op jit(solution)/shard_map/ppermute | solution.py:317
  69.4 3.8 %collective-permute-start.17 = (f32[3,128,256]{2,1,0:T(8,128)}, f32[3,128,256]{2,1,0:T(8,128)S(1)}, u32[]{:S(2)}, u32[]{:S(2)}) collective-permute-start(f32[3,128,256]{2,1,0:T(8,128)} %share.1.refs_1_), channel_id=1, source_target_pairs={{0,8},{8,16},{16,24},{24,28},{28,20},{20,12},{12,4},{4,0},{1,9},{9... | collective-permute-start | bytes 1179656 | tf_op jit(solution)/shard_map/ppermute | solution.py:340
  73.2 6.8 %collective-permute-done.17.refs_0_ = f32[3,128,256]{2,1,0:T(8,128)S(1)} collective-permute-done((f32[3,128,256]{2,1,0:T(8,128)}, f32[3,128,256]{2,1,0:T(8,128)S(1)}, u32[]{:S(2)}, u32[]{:S(2)}) %collective-permute-start.17) | collective-permute-done | bytes 393248 | tf_op jit(solution)/shard_map/ppermute | solution.py:340
  83.5 5.8 %collective-permute-done.18.refs_2_ = f32[3,128,256]{2,1,0:T(8,128)S(1)} collective-permute-done((f32[3,128,256]{2,1,0:T(8,128)S(1)}, f32[3,128,256]{2,1,0:T(8,128)S(1)}, u32[]{:S(2)}, u32[]{:S(2)}) %collective-permute-start.18) | collective-permute-done | bytes 393248 | tf_op jit(solution)/shard_map/ppermute | solution.py:340
  93.4 6.0 %collective-permute-done.19.refs_1_ = f32[3,128,256]{2,1,0:T(8,128)S(1)} collective-permute-done((f32[3,128,256]{2,1,0:T(8,128)S(1)}, f32[3,128,256]{2,1,0:T(8,128)S(1)}, u32[]{:S(2)}, u32[]{:S(2)}) %collective-permute-start.19) | collective-permute-done | bytes 393248 | tf_op jit(solution)/shard_map/ppermute | solution.py:340
  103.5 7.3 %collective-permute-done.20.refs_1_ = f32[3,128,256]{2,1,0:T(8,128)S(1)} collective-permute-done((f32[3,128,256]{2,1,0:T(8,128)S(1)}, f32[3,128,256]{2,1,0:T(8,128)S(1)}, u32[]{:S(2)}, u32[]{:S(2)}) %collective-permute-start.20) | collective-permute-done | bytes 393248 | tf_op jit(solution)/shard_map/ppermute | solution.py:340
  114.9 7.7 %collective-permute-done.21.refs_1_ = f32[3,128,256]{2,1,0:T(8,128)S(1)} collective-permute-done((f32[3,128,256]{2,1,0:T(8,128)S(1)}, f32[3,128,256]{2,1,0:T(8,128)S(1)}, u32[]{:S(2)}, u32[]{:S(2)}) %collective-permute-start.21) | collective-permute-done | bytes 393248 | tf_op jit(solution)/shard_map/ppermute | solution.py:340
  129.3 5.0 %collective-permute-done.22.refs_1_ = f32[3,128,256]{2,1,0:T(8,128)S(1)} collective-permute-done((f32[3,128,256]{2,1,0:T(8,128)S(1)}, f32[3,128,256]{2,1,0:T(8,128)S(1)}, u32[]{:S(2)}, u32[]{:S(2)}) %collective-permute-start.22) | collective-permute-done | bytes 393248 | tf_op jit(solution)/shard_map/ppermute | solution.py:340
  138.2 5.4 %order.1.plan_ref = s32[104]{0:T(128)} custom-call(s32[86]{0:T(128)} %cols_ref.3, s32[1,16]{1,0:T(1,128)} %counts_ref, s32[3]{0:T(128)} %get-tuple-element.20.heavy_ref.refs_0_), custom_call_target="tpu_custom_call" | custom-call | tf_op jit(solution)/shard_map/order/pallas_call | solution.py:208
  145.2 2.6 %copy-done.2 = f32[86,128,128]{2,1,0:T(8,128)S(1)} copy-done((f32[86,128,128]{2,1,0:T(8,128)S(1)}, f32[86,128,128]{2,1,0:T(8,128)}, u32[]{:S(2)}) %copy-start.2) | copy-done | bytes 5636120
  148.4 6.3 %add.27 = (f32[16,128,256]{2,1,0:T(8,128)S(1)}, f32[86,128,128]{2,1,0:T(8,128)S(1)}) custom-call(s32[104]{0:T(128)S(1)} %copy-done.23, f32[86,128,128]{2,1,0:T(8,128)S(1)} %copy-done.2, f32[16,128,256]{2,1,0:T(8,128)S(1)} %bitcast.9, f32[3,128,256]{2,1,0:T(8,128)} %share.1.refs_1_), custom_call_target="tpu_custom_call" | custom-call | flops 167772160 | bytes 2097152 | tf_op jit(solution)/shard_map/add/pallas_call | solution.py:284
  154.7 2.8 %add.28.refs_3_ = f32[16,128,256]{2,1,0:T(8,128)S(1)} custom-call(s32[104]{0:T(128)S(1)} %copy-done.23, f32[86,128,128]{2,1,0:T(8,128)S(1)} %get-tuple-element.30.tiles_ref, f32[3,128,256]{2,1,0:T(8,128)S(1)} %copy-done.6, f32[3,128,256]{2,1,0:T(8,128)} %collective-permute-done.24.refs_1_, ...), custom_call_target="tpu_custom_call", output_to_operand_aliasing={{}: (4, {})} | custom-call | flops 167772160 | bytes 2097152 | tf_op jit(solution)/shard_map/add/pallas_call | solution.py:284
  166.7 2.5 %add.33.refs_2_ = f32[16,128,256]{2,1,0:T(8,128)S(1)} custom-call(s32[104]{0:T(128)S(1)} %copy-done.23, f32[86,128,128]{2,1,0:T(8,128)S(1)} %get-tuple-element.30.tiles_ref, f32[3,128,256]{2,1,0:T(8,128)S(1)} %copy-done.20, f32[3,128,256]{2,1,0:T(8,128)S(1)} %copy-done.22, f32[16,128,256]{2,1,0:T(8,128)S(1)} %add.32.refs_2_), custom_call_target="tpu_custom_call", output_to_operand_aliasing={{}: (4, {})} | custom-call | flops 167772160 | bytes 2097152 | tf_op jit(solution)/shard_map/add/pallas_call | solution.py:284
  169.2 2.5 %add.34.refs_1_ = f32[16,128,256]{2,1,0:T(8,128)S(1)} custom-call(s32[104]{0:T(128)S(1)} %copy-done.23, f32[86,128,128]{2,1,0:T(8,128)S(1)} %get-tuple-element.30.tiles_ref, f32[3,128,256]{2,1,0:T(8,128)} %collective-permute-done.15.refs_0_, f32[3,128,256]{2,1,0:T(8,128)} %collective-permute-done.23.refs_1_, ...), custom_call_target="tpu_custom_call", output_to_operand_aliasing={{}: (4, {})} | custom-call | flops 167772160 | bytes 2097152 | tf_op jit(solution)/shard_map/add/pallas_call | solution.py:284
  173.8 5.2 %all-gather = f32[4,1,2048]{2,1,0:T(1,128)S(1)} all-gather(f32[1,1,2048]{2,1,0:T(1,128)S(1)} %bitcast.10), channel_id=1, replica_groups=mesh['rows'=8,'feat'=4] {'feat'}, dimensions={0}, use_global_device_ids=true | all-gather | bytes 40960 | tf_op jit(solution)/shard_map/all_gather | solution.py:378
  (108 shorter events, 60.5 us)
Async XLA Ops:
  3.6 4.8 %collective-permute-start.7 = (s32[8,8]{1,0:T(8,128)}, s32[8,8]{1,0:T(8,128)S(1)}, u32[]{:S(2)}, u32[]{:S(2)}) collective-permute-start(s32[8,8]{1,0:T(8,128)} %get-tuple-element.32), channel_id=1, source_target_pairs={{0,4},{4,0},{8,12},{12,8},{16,20},{20,16},{24,28},{28,24},{1,5},{5... | collective-permute-start | bytes 776 | tf_op jit(solution)/shard_map/ppermute | solution.py:318
  9.1 5.7 %collective-permute-start.10 = (s32[8,8]{1,0:T(8,128)S(1)}, s32[8,8]{1,0:T(8,128)S(1)}, u32[]{:S(2)}, u32[]{:S(2)}) collective-permute-start(s32[8,8]{1,0:T(8,128)S(1)} %add.22.refs_1_), channel_id=1, source_target_pairs={{0,24},{4,28},{8,16},{12,20},{16,8},{20,12},{24,0},{28,4},{1,25},{... | collective-permute-start | bytes 776 | tf_op jit(solution)/shard_map/ppermute | solution.py:318
  20.2 62.2 %all-to-all-start = ((f32[8,128,256]{2,1,0:T(8,128)}), f32[8,128,256]{2,1,0:T(8,128)S(1)}, u32[]{:S(2)}, u32[]{:S(2)}) async-start(f32[8,128,256]{2,1,0:T(8,128)} %pick.2), calls=%async_computation | async-start | bytes 2097152 | tf_op jit(solution)/shard_map/all_to_all | solution.py:329
  24.4 10.2 %collective-permute-start = (f32[128,256]{1,0:T(8,128)}, f32[128,256]{1,0:T(8,128)S(1)}, u32[]{:S(2)}, u32[]{:S(2)}) collective-permute-start(f32[128,256]{1,0:T(8,128)} %copy-done.28), channel_id=1, source_target_pairs={{0,4},{4,0},{8,12},{12,8},{16,20},{20,16},{24,28},{28,24},{1,5},{5... | collective-permute-start | bytes 393224 | tf_op jit(solution)/shard_map/ppermute | solution.py:317
  26.4 19.2 %collective-permute-start.1 = (f32[128,256]{1,0:T(8,128)}, f32[128,256]{1,0:T(8,128)S(1)}, u32[]{:S(2)}, u32[]{:S(2)}) collective-permute-start(f32[128,256]{1,0:T(8,128)} %copy-done.27), channel_id=1, source_target_pairs={{0,8},{4,12},{8,0},{12,4},{16,24},{20,28},{24,16},{28,20},{1,9},{5... | collective-permute-start | bytes 393224 | tf_op jit(solution)/shard_map/ppermute | solution.py:317
  27.9 22.3 %collective-permute-start.2 = (f32[128,256]{1,0:T(8,128)}, f32[128,256]{1,0:T(8,128)S(1)}, u32[]{:S(2)}, u32[]{:S(2)}) collective-permute-start(f32[128,256]{1,0:T(8,128)} %copy-done.26), channel_id=1, source_target_pairs={{0,12},{4,8},{8,4},{12,0},{16,28},{20,24},{24,20},{28,16},{1,13},{... | collective-permute-start | bytes 393224 | tf_op jit(solution)/shard_map/ppermute | solution.py:317
  27.9 36.3 %collective-permute-start.3 = (f32[128,256]{1,0:T(8,128)}, f32[128,256]{1,0:T(8,128)S(1)}, u32[]{:S(2)}, u32[]{:S(2)}) collective-permute-start(f32[128,256]{1,0:T(8,128)} %copy-done.25), channel_id=1, source_target_pairs={{0,16},{4,20},{8,24},{12,28},{16,0},{20,4},{24,8},{28,12},{1,17},{... | collective-permute-start | bytes 393224 | tf_op jit(solution)/shard_map/ppermute | solution.py:317
  30.8 36.7 %collective-permute-start.4 = (f32[128,256]{1,0:T(8,128)S(1)}, f32[128,256]{1,0:T(8,128)S(1)}, u32[]{:S(2)}, u32[]{:S(2)}) collective-permute-start(f32[128,256]{1,0:T(8,128)S(1)} %get-tuple-element.25), channel_id=1, source_target_pairs={{0,20},{4,16},{8,28},{12,24},{16,4},{20,0},{24,12},{28,8},{1,21},{... | collective-permute-start | bytes 393224 | tf_op jit(solution)/shard_map/ppermute | solution.py:317
  34.6 32.9 %collective-permute-start.5 = (f32[128,256]{1,0:T(8,128)S(1)}, f32[128,256]{1,0:T(8,128)S(1)}, u32[]{:S(2)}, u32[]{:S(2)}) collective-permute-start(f32[128,256]{1,0:T(8,128)S(1)} %get-tuple-element.26), channel_id=1, source_target_pairs={{0,24},{4,28},{8,16},{12,20},{16,8},{20,12},{24,0},{28,4},{1,25},{... | collective-permute-start | bytes 393224 | tf_op jit(solution)/shard_map/ppermute | solution.py:317
  45.6 21.9 %collective-permute-start.6 = (f32[128,256]{1,0:T(8,128)S(1)}, f32[128,256]{1,0:T(8,128)S(1)}, u32[]{:S(2)}, u32[]{:S(2)}) collective-permute-start(f32[128,256]{1,0:T(8,128)S(1)} %get-tuple-element.27), channel_id=1, source_target_pairs={{0,28},{4,24},{8,20},{12,16},{16,12},{20,8},{24,4},{28,0},{1,29},{... | collective-permute-start | bytes 393224 | tf_op jit(solution)/shard_map/ppermute | solution.py:317
  69.4 10.6 %collective-permute-start.17 = (f32[3,128,256]{2,1,0:T(8,128)}, f32[3,128,256]{2,1,0:T(8,128)S(1)}, u32[]{:S(2)}, u32[]{:S(2)}) collective-permute-start(f32[3,128,256]{2,1,0:T(8,128)} %share.1.refs_1_), channel_id=1, source_target_pairs={{0,8},{8,16},{16,24},{24,28},{28,20},{20,12},{12,4},{4,0},{1,9},{9... | collective-permute-start | bytes 1179656 | tf_op jit(solution)/shard_map/ppermute | solution.py:340
  80.0 9.3 %collective-permute-start.18 = (f32[3,128,256]{2,1,0:T(8,128)S(1)}, f32[3,128,256]{2,1,0:T(8,128)S(1)}, u32[]{:S(2)}, u32[]{:S(2)}) collective-permute-start(f32[3,128,256]{2,1,0:T(8,128)S(1)} %collective-permute-done.17.refs_0_), channel_id=1, source_target_pairs={{0,8},{8,16},{16,24},{24,28},{28,20},{20,12},{12,4},{4,0},{1,9},{9... | collective-permute-start | bytes 1179656 | tf_op jit(solution)/shard_map/ppermute | solution.py:340
  83.5 9.0 %collective-permute-start.11 = (f32[3,128,256]{2,1,0:T(8,128)S(1)}, f32[3,128,256]{2,1,0:T(8,128)S(1)}, u32[]{:S(2)}, u32[]{:S(2)}) collective-permute-start(f32[3,128,256]{2,1,0:T(8,128)S(1)} %pick.3.refs_1_), channel_id=1, source_target_pairs={{8,0},{16,8},{24,16},{28,24},{20,28},{12,20},{4,12},{0,4},{9,1},{1... | collective-permute-start | bytes 1179656 | tf_op jit(solution)/shard_map/ppermute | solution.py:340
  89.3 10.2 %collective-permute-start.19 = (f32[3,128,256]{2,1,0:T(8,128)S(1)}, f32[3,128,256]{2,1,0:T(8,128)S(1)}, u32[]{:S(2)}, u32[]{:S(2)}) collective-permute-start(f32[3,128,256]{2,1,0:T(8,128)S(1)} %collective-permute-done.18.refs_2_), channel_id=1, source_target_pairs={{0,8},{8,16},{16,24},{24,28},{28,20},{20,12},{12,4},{4,0},{1,9},{9... | collective-permute-start | bytes 1179656 | tf_op jit(solution)/shard_map/ppermute | solution.py:340
  92.4 10.2 %collective-permute-start.12 = (f32[3,128,256]{2,1,0:T(8,128)S(1)}, f32[3,128,256]{2,1,0:T(8,128)S(1)}, u32[]{:S(2)}, u32[]{:S(2)}) collective-permute-start(f32[3,128,256]{2,1,0:T(8,128)S(1)} %collective-permute-done.11.refs_0_), channel_id=1, source_target_pairs={{8,0},{16,8},{24,16},{28,24},{20,28},{12,20},{4,12},{0,4},{9,1},{1... | collective-permute-start | bytes 1179656 | tf_op jit(solution)/shard_map/ppermute | solution.py:340
  99.5 11.3 %collective-permute-start.20 = (f32[3,128,256]{2,1,0:T(8,128)S(1)}, f32[3,128,256]{2,1,0:T(8,128)S(1)}, u32[]{:S(2)}, u32[]{:S(2)}) collective-permute-start(f32[3,128,256]{2,1,0:T(8,128)S(1)} %collective-permute-done.19.refs_1_), channel_id=1, source_target_pairs={{0,8},{8,16},{16,24},{24,28},{28,20},{20,12},{12,4},{4,0},{1,9},{9... | collective-permute-start | bytes 1179656 | tf_op jit(solution)/shard_map/ppermute | solution.py:340
  102.7 11.3 %collective-permute-start.13 = (f32[3,128,256]{2,1,0:T(8,128)S(1)}, f32[3,128,256]{2,1,0:T(8,128)S(1)}, u32[]{:S(2)}, u32[]{:S(2)}) collective-permute-start(f32[3,128,256]{2,1,0:T(8,128)S(1)} %collective-permute-done.12.refs_0_), channel_id=1, source_target_pairs={{8,0},{16,8},{24,16},{28,24},{20,28},{12,20},{4,12},{0,4},{9,1},{1... | collective-permute-start | bytes 1179656 | tf_op jit(solution)/shard_map/ppermute | solution.py:340
  110.7 11.9 %collective-permute-start.21 = (f32[3,128,256]{2,1,0:T(8,128)S(1)}, f32[3,128,256]{2,1,0:T(8,128)S(1)}, u32[]{:S(2)}, u32[]{:S(2)}) collective-permute-start(f32[3,128,256]{2,1,0:T(8,128)S(1)} %collective-permute-done.20.refs_1_), channel_id=1, source_target_pairs={{0,8},{8,16},{16,24},{24,28},{28,20},{20,12},{12,4},{4,0},{1,9},{9... | collective-permute-start | bytes 1179656 | tf_op jit(solution)/shard_map/ppermute | solution.py:340
  114.0 12.0 %collective-permute-start.14 = (f32[3,128,256]{2,1,0:T(8,128)S(1)}, f32[3,128,256]{2,1,0:T(8,128)S(1)}, u32[]{:S(2)}, u32[]{:S(2)}) collective-permute-start(f32[3,128,256]{2,1,0:T(8,128)S(1)} %collective-permute-done.13.refs_0_), channel_id=1, source_target_pairs={{8,0},{16,8},{24,16},{28,24},{20,28},{12,20},{4,12},{0,4},{9,1},{1... | collective-permute-start | bytes 1179656 | tf_op jit(solution)/shard_map/ppermute | solution.py:340
  122.6 11.8 %collective-permute-start.22 = (f32[3,128,256]{2,1,0:T(8,128)S(1)}, f32[3,128,256]{2,1,0:T(8,128)S(1)}, u32[]{:S(2)}, u32[]{:S(2)}) collective-permute-start(f32[3,128,256]{2,1,0:T(8,128)S(1)} %collective-permute-done.21.refs_1_), channel_id=1, source_target_pairs={{0,8},{8,16},{16,24},{24,28},{28,20},{20,12},{12,4},{4,0},{1,9},{9... | collective-permute-start | bytes 1179656 | tf_op jit(solution)/shard_map/ppermute | solution.py:340
  125.9 12.1 %collective-permute-start.15 = (f32[3,128,256]{2,1,0:T(8,128)S(1)}, f32[3,128,256]{2,1,0:T(8,128)}, u32[]{:S(2)}, u32[]{:S(2)}) collective-permute-start(f32[3,128,256]{2,1,0:T(8,128)S(1)} %collective-permute-done.14.refs_0_), channel_id=1, source_target_pairs={{8,0},{16,8},{24,16},{28,24},{20,28},{12,20},{4,12},{0,4},{9,1},{1... | collective-permute-start | bytes 1179656 | tf_op jit(solution)/shard_map/ppermute | solution.py:340
  126.9 27.8 %collective-permute-start.24 = (f32[3,128,256]{2,1,0:T(8,128)}, f32[3,128,256]{2,1,0:T(8,128)}, u32[]{:S(2)}, u32[]{:S(2)}) collective-permute-start(f32[3,128,256]{2,1,0:T(8,128)} %share.1.refs_1_), channel_id=1, source_target_pairs={{8,0},{16,8},{24,16},{28,24},{20,28},{12,20},{4,12},{0,4},{9,1},{1... | collective-permute-start | bytes 1179656 | tf_op jit(solution)/shard_map/ppermute | solution.py:340
  135.1 34.1 %collective-permute-start.23 = (f32[3,128,256]{2,1,0:T(8,128)S(1)}, f32[3,128,256]{2,1,0:T(8,128)}, u32[]{:S(2)}, u32[]{:S(2)}) collective-permute-start(f32[3,128,256]{2,1,0:T(8,128)S(1)} %pick.3.refs_1_), channel_id=1, source_target_pairs={{0,8},{8,16},{16,24},{24,28},{28,20},{20,12},{12,4},{4,0},{1,9},{9... | collective-permute-start | bytes 1179656 | tf_op jit(solution)/shard_map/ppermute | solution.py:340
  138.0 33.7 %collective-permute-start.16 = (f32[3,128,256]{2,1,0:T(8,128)}, f32[3,128,256]{2,1,0:T(8,128)}, u32[]{:S(2)}, u32[]{:S(2)}) collective-permute-start(f32[3,128,256]{2,1,0:T(8,128)} %collective-permute-done.15.refs_0_), channel_id=1, source_target_pairs={{8,0},{16,8},{24,16},{28,24},{20,28},{12,20},{4,12},{0,4},{9,1},{1... | collective-permute-start | bytes 1179656 | tf_op jit(solution)/shard_map/ppermute | solution.py:340
  (32 other events, 228.4 us)

commit v4 on v3

--- a/solution.py
+++ b/solution.py
@@ -77,11 +77,28 @@
     )(tile_cols)
 
 
-def head_kernel(n, blocks_dev, tile_total, cols_ref, from_ref, heavy_ref, mine_ref, want_ref, *refs):
-    letters, (seen_ref, last_ref, sem_ref) = refs[: n - 1], refs[n - 1:]
+def letters_kernel(n, from_ref, *refs):
+    letters, sem_ref = refs[: n - 1], refs[n - 1]
     copies = [pltpu.make_async_copy(from_ref.at[m], letters[m - 1], sem_ref.at[m - 1]) for m in range(1, n)]
     for copy in copies:
         copy.start()
+    for copy in copies:
+        copy.wait()
+
+
+def write_letters(n, blocks):
+    return pl.pallas_call(
+        functools.partial(letters_kernel, n),
+        out_shape=[pltpu.VMEM(blocks.shape[1:], jnp.float32)] * (n - 1),
+        in_specs=[HBM],
+        out_specs=[VMEM] * (n - 1),
+        scratch_shapes=[pltpu.SemaphoreType.DMA((n - 1,))],
+        compiler_params=pltpu.CompilerParams(vmem_limit_bytes=58 << 20),
+        name="letters",
+    )(pltpu.with_memory_space_constraint(blocks, pltpu.HBM))
+
+
+def asks_kernel(n, blocks_dev, tile_total, cols_ref, heavy_ref, mine_ref, want_ref, seen_ref, last_ref):
     me = lax.axis_index("rows")
     for o in range(n):
         for p in range(n):
@@ -89,32 +106,23 @@
     find_heavy(n, blocks_dev, tile_total, cols_ref, heavy_ref, mine_ref, seen_ref, last_ref)
     for p in range(n):
         want_ref[me, p] = last_ref[p]
-    for copy in copies:
-        copy.wait()
-
-
-def start_up(n, blocks_dev, tile_cols, blocks):
+
+
+def find_asks(n, blocks_dev, tile_cols):
     tile_total = tile_cols.shape[0]
-    letter = pltpu.VMEM(blocks.shape[1:], jnp.float32)
-    heavy_ids, mine, want, *letters = pl.pallas_call(
-        functools.partial(head_kernel, n, blocks_dev, tile_total),
+    return pl.pallas_call(
+        functools.partial(asks_kernel, n, blocks_dev, tile_total),
         out_shape=(
             jax.ShapeDtypeStruct((HEAVY,), jnp.int32),
             jax.ShapeDtypeStruct((1,), jnp.int32),
             jax.ShapeDtypeStruct((n, n), jnp.int32),
-            *[letter] * (n - 1),
         ),
-        in_specs=[SMEM, HBM],
-        out_specs=(SMEM, SMEM, SMEM, *[VMEM] * (n - 1)),
-        scratch_shapes=[
-            pltpu.SMEM((n,), jnp.int32),
-            pltpu.SMEM((n,), jnp.int32),
-            pltpu.SemaphoreType.DMA((n - 1,)),
-        ],
-        compiler_params=pltpu.CompilerParams(vmem_limit_bytes=58 << 20),
-        name="head",
-    )(tile_cols, pltpu.with_memory_space_constraint(blocks, pltpu.HBM))
-    return heavy_ids, mine, want, letters
+        in_specs=[SMEM],
+        out_specs=(SMEM,) * 3,
+        scratch_shapes=[pltpu.SMEM((n,), jnp.int32), pltpu.SMEM((n,), jnp.int32)],
+        compiler_params=pltpu.CompilerParams(vmem_limit_bytes=8 << 20),
+        name="asks",
+    )(tile_cols)
 
 
 def share_kernel(n, home, heavy_ref, from_ref, *refs):
@@ -171,7 +179,9 @@
                 there = ring_place(jnp.where(half == 0, owner ^ (local % n), local % n), n)
                 hops = jnp.where(half == 0, here - there, there - here)
                 hops = jnp.where(hops < 0, hops + n, hops)
-                heavy_list, heavy_slot = 2 + 2 * hops + half, heavy_at
+                single = (half == 1) & (hops == n - 2) & (heavy_at == HEAVY - 1)
+                heavy_list = jnp.where(single, 2 * n + 2, 2 + 2 * hops + half)
+                heavy_slot = jnp.where(single, 0, heavy_at)
             else:
                 heavy_list, heavy_slot = 2, heavy_at * blocks_dev + local
             own = owner == me
@@ -310,11 +320,12 @@
     swap = functools.partial(lax.all_to_all, axis_name="rows", split_axis=0, concat_axis=0, tiled=True)
     tie = lax.optimization_barrier
     if ring:
-        lists = 2 + 2 * n
-        heavy_ids, mine, want, letters = start_up(n, blocks_dev, tile_cols, blocks)
+        lists = 3 + 2 * n
+        letters = write_letters(n, blocks)
         got = {}
         for m in (*range(n // 2, n), *range(1, n // 2)):
             got[m] = lax.ppermute(letters[m - 1], "rows", [(i, i ^ m) for i in range(n)])
+        heavy_ids, mine, want = find_asks(n, blocks_dev, tile_cols)
         flip = lambda x, m: lax.ppermute(x, "rows", [(i, i ^ m) for i in range(n)])
         want = [want, flip(want, 1)]
         pair = want[0] + want[1]
@@ -361,10 +372,14 @@
             elif hop == n - 3:
                 mine_back, ahead = tie((mine_back, ahead))
                 ahead = hop_on("up", mine_back)
-            back = hop_on("down", back)
+            if hop < n - 2:
+                back = hop_on("down", back)
+            else:
+                last = hop_on("up", ahead[HEAVY - 1:])
+                back = hop_on("down", back[: HEAVY - 1])
             sums = add_now(ready, *sums)
             ready = [(3 + 2 * hop, back)]
-        _, total = add_now(ready, *sums)
+        _, total = add_now([*ready, (2 * n + 2, last)], *sums)
     else:
         heavy_ids, _, want = find_wants(n, blocks_dev, tile_cols)
         asked = swap(want.reshape(n, 1))[:, 0]
@@ -375,7 +390,11 @@
         heavy = lax.all_gather(scattered, "rows", axis=1, tiled=True).reshape(HEAVY * blocks_dev, block, width)
         total, _ = add_products(plan, tile_values, (0, 1, 2), (blocks, light, heavy), None, blocks_dev, slots)
     aggregate = total.reshape(node_dev, width)
-    square_sum = jnp.sum(lax.all_gather(jnp.sum(aggregate * aggregate, axis=1), "feat"), axis=0)
+    squares = jnp.sum(aggregate * aggregate, axis=1)
+    parts = lax.axis_size("feat")
+    square_sum = squares
+    for shift in range(1, parts):
+        square_sum += lax.ppermute(squares, "feat", [(i, (i + shift) % parts) for i in range(parts)])
     mean_square = square_sum / (width * lax.axis_size("feat"))
     return aggregate * norm_gain[None, :] * lax.rsqrt(mean_square + 1e-05)[:, None]
 

time: 181 us -> 183 us (1.011)
  blocking collectives: 5.19 us -> 0 us
  starting transfers between devices: 49.3 us -> 53.7 us
  local copies, waits for them, and re-layouts: 12.3 us -> 14.9 us
    all_gather x1 -> x0, blocking collectives: 5.19 us -> none  [per_device(): lax.all_gather(jnp.sum(aggregate * aggregate, axis=1), 'feat')]
    ppermute x0 -> x3, starting transfers between devices: none -> 3.03 us  [per_device(): lax.ppermute(squares, 'feat', [(i, (i + shift) % parts) for i in range(pa...]
    pallas_call x1 -> x2, Pallas kernels: 2.96 us -> 3.97 us  [the longest x1 2.67 us: find_asks(): pl.pallas_call(functools.partial(asks_kernel, n, blocks_dev, tile_total),...]
    unnamed x60 -> x54, local copies, waits for them, and re-layouts: 12.3 us -> 13.3 us
    ppermute x14 -> x15, starting transfers between devices: 21.6 us -> 22.6 us  [hop_on(): return lax.ppermute(x, 'rows', up if way == 'up' else down)]
    ppermute x14 -> x15, waiting for transfers between devices: 39.3 us -> 40.3 us  [hop_on(): return lax.ppermute(x, 'rows', up if way == 'up' else down)]
  transfers between devices with their start and end apart: 26 -> 30, of which waited for: 17 -> 19; matrix products, arithmetic and copies ran while one was open for 0% -> 1% of each run, Pallas kernels for 17% -> 18%
where the time goes in v4:
time: 183 us
  waiting for transfers between devices  72.9 us (40%)
  starting transfers between devices  53.7 us (29%)
  Pallas kernels  38.8 us (21%)
  local copies, waits for them, and re-layouts  14.9 us (8%)
  other arithmetic  2.02 us (1%)
    ppermute x15, waiting for transfers between devices, hop_on(): return lax.ppermute(x, 'rows', up if way == 'up' else down)  40.3 us
    ppermute x7, waiting for transfers between devices, per_device(): lax.ppermute(letters[m - 1], 'rows', [(i, i ^ m) for i in range(n)])  25.8 us
    pallas_call x9, Pallas kernels, add_products(): pl.pallas_call(functools.partial(add_kernel, lists, plan.shape[0] - tile_...  24.6 us
    ppermute x15, starting transfers between devices, hop_on(): return lax.ppermute(x, 'rows', up if way == 'up' else down)  22.6 us
    ppermute x7, starting transfers between devices, per_device(): lax.ppermute(letters[m - 1], 'rows', [(i, i ^ m) for i in range(n)])  16 us
    unnamed x54, local copies, waits for them, and re-layouts  13.3 us
    ppermute x4, starting transfers between devices, per_device(): flip = lambda x, m: lax.ppermute(x, 'rows', [(i, i ^ m) for i in range(n)])  7.73 us
    ppermute x4, waiting for transfers between devices, per_device(): flip = lambda x, m: lax.ppermute(x, 'rows', [(i, i ^ m) for i in range(n)])  5.53 us
  transfers between devices with their start and end apart: 30, of which 19 were waited for; matrix products, arithmetic and copies ran while one was open for 1% of the time, Pallas kernels for 18%

profile of v4, /device:TPU:0, one launch (start us, length us, event | category | flops | bytes accessed | tf_op | source)
XLA Modules:
  0.0 182.8 jit_solution(12973017793223122492)
XLA Ops:
  0.7 2.7 %asks.1 = (s32[3]{0:T(128)S(1)}, s32[1]{0:T(128)}, s32[8,8]{1,0:T(8,128)S(1)}) custom-call(s32[86]{0:T(128)S(1)} %copy-done.25), custom_call_target="tpu_custom_call" | custom-call | tf_op jit(solution)/shard_map/asks/pallas_call | solution.py:113
  3.3 3.0 %collective-permute-start.7 = (s32[8,8]{1,0:T(8,128)S(1)}, s32[8,8]{1,0:T(8,128)S(1)}, u32[]{:S(2)}, u32[]{:S(2)}) collective-permute-start(s32[8,8]{1,0:T(8,128)S(1)} %get-tuple-element.32), channel_id=1, source_target_pairs={{0,4},{4,0},{8,12},{12,8},{16,20},{20,16},{24,28},{28,24},{1,5},{5... | collective-permute-start | bytes 776 | tf_op jit(solution)/shard_map/ppermute | solution.py:329
  8.0 4.1 %collective-permute-start.10 = (s32[8,8]{1,0:T(8,128)S(1)}, s32[8,8]{1,0:T(8,128)S(1)}, u32[]{:S(2)}, u32[]{:S(2)}) collective-permute-start(s32[8,8]{1,0:T(8,128)S(1)} %add.27.refs_1_), channel_id=1, source_target_pairs={{0,24},{4,28},{8,16},{12,20},{16,8},{20,12},{24,0},{28,4},{1,25},{... | collective-permute-start | bytes 776 | tf_op jit(solution)/shard_map/ppermute | solution.py:329
  20.7 4.4 %all-to-all-start = ((f32[8,128,256]{2,1,0:T(8,128)}), f32[8,128,256]{2,1,0:T(8,128)S(1)}, u32[]{:S(2)}, u32[]{:S(2)}) async-start(f32[8,128,256]{2,1,0:T(8,128)} %pick.2), calls=%async_computation | async-start | bytes 2097152 | tf_op jit(solution)/shard_map/all_to_all | solution.py:340
  30.0 2.8 %collective-permute-start.3 = (f32[128,256]{1,0:T(8,128)S(1)}, f32[128,256]{1,0:T(8,128)S(1)}, u32[]{:S(2)}, u32[]{:S(2)}) collective-permute-start(f32[128,256]{1,0:T(8,128)S(1)} %get-tuple-element.24), channel_id=1, source_target_pairs={{0,16},{4,20},{8,24},{12,28},{16,0},{20,4},{24,8},{28,12},{1,17},{... | collective-permute-start | bytes 393224 | tf_op jit(solution)/shard_map/ppermute | solution.py:327
  35.2 3.4 %collective-permute-start.5 = (f32[128,256]{1,0:T(8,128)S(1)}, f32[128,256]{1,0:T(8,128)S(1)}, u32[]{:S(2)}, u32[]{:S(2)}) collective-permute-start(f32[128,256]{1,0:T(8,128)S(1)} %get-tuple-element.26), channel_id=1, source_target_pairs={{0,24},{4,28},{8,16},{12,20},{16,8},{20,12},{24,0},{28,4},{1,25},{... | collective-permute-start | bytes 393224 | tf_op jit(solution)/shard_map/ppermute | solution.py:327
  38.6 7.6 %collective-permute-done.1.refs_1_ = f32[128,256]{1,0:T(8,128)S(1)} collective-permute-done((f32[128,256]{1,0:T(8,128)S(1)}, f32[128,256]{1,0:T(8,128)S(1)}, u32[]{:S(2)}, u32[]{:S(2)}) %collective-permute-start.1) | collective-permute-done | bytes 131104 | tf_op jit(solution)/shard_map/ppermute | solution.py:327
  46.1 4.6 %collective-permute-start.6 = (f32[128,256]{1,0:T(8,128)S(1)}, f32[128,256]{1,0:T(8,128)S(1)}, u32[]{:S(2)}, u32[]{:S(2)}) collective-permute-start(f32[128,256]{1,0:T(8,128)S(1)} %get-tuple-element.27), channel_id=1, source_target_pairs={{0,28},{4,24},{8,20},{12,16},{16,12},{20,8},{24,4},{28,0},{1,29},{... | collective-permute-start | bytes 393224 | tf_op jit(solution)/shard_map/ppermute | solution.py:327
  50.8 14.1 %collective-permute-done.3.refs_3_ = f32[128,256]{1,0:T(8,128)S(1)} collective-permute-done((f32[128,256]{1,0:T(8,128)S(1)}, f32[128,256]{1,0:T(8,128)S(1)}, u32[]{:S(2)}, u32[]{:S(2)}) %collective-permute-start.3) | collective-permute-done | bytes 131104 | tf_op jit(solution)/shard_map/ppermute | solution.py:327
  64.8 3.3 %collective-permute-done.4.refs_4_ = f32[128,256]{1,0:T(8,128)S(1)} collective-permute-done((f32[128,256]{1,0:T(8,128)S(1)}, f32[128,256]{1,0:T(8,128)S(1)}, u32[]{:S(2)}, u32[]{:S(2)}) %collective-permute-start.4) | collective-permute-done | bytes 131104 | tf_op jit(solution)/shard_map/ppermute | solution.py:327
  69.4 3.8 %collective-permute-start.17 = (f32[3,128,256]{2,1,0:T(8,128)S(1)}, f32[3,128,256]{2,1,0:T(8,128)}, u32[]{:S(2)}, u32[]{:S(2)}) collective-permute-start(f32[3,128,256]{2,1,0:T(8,128)S(1)} %share.1.refs_1_), channel_id=1, source_target_pairs={{0,8},{8,16},{16,24},{24,28},{28,20},{20,12},{12,4},{4,0},{1,9},{9... | collective-permute-start | bytes 1179656 | tf_op jit(solution)/shard_map/ppermute | solution.py:351
  73.2 6.4 %collective-permute-done.17.refs_0_ = f32[3,128,256]{2,1,0:T(8,128)} collective-permute-done((f32[3,128,256]{2,1,0:T(8,128)S(1)}, f32[3,128,256]{2,1,0:T(8,128)}, u32[]{:S(2)}, u32[]{:S(2)}) %collective-permute-start.17) | collective-permute-done | bytes 393248 | tf_op jit(solution)/shard_map/ppermute | solution.py:351
  79.5 2.6 %collective-permute-start.18 = (f32[3,128,256]{2,1,0:T(8,128)}, f32[3,128,256]{2,1,0:T(8,128)}, u32[]{:S(2)}, u32[]{:S(2)}) collective-permute-start(f32[3,128,256]{2,1,0:T(8,128)} %collective-permute-done.17.refs_0_), channel_id=1, source_target_pairs={{0,8},{8,16},{16,24},{24,28},{28,20},{20,12},{12,4},{4,0},{1,9},{9... | collective-permute-start | bytes 1179656 | tf_op jit(solution)/shard_map/ppermute | solution.py:351
  83.3 5.6 %collective-permute-done.18.refs_2_ = f32[3,128,256]{2,1,0:T(8,128)} collective-permute-done((f32[3,128,256]{2,1,0:T(8,128)}, f32[3,128,256]{2,1,0:T(8,128)}, u32[]{:S(2)}, u32[]{:S(2)}) %collective-permute-start.18) | collective-permute-done | bytes 393248 | tf_op jit(solution)/shard_map/ppermute | solution.py:351
  92.9 6.1 %collective-permute-done.19.refs_1_ = f32[3,128,256]{2,1,0:T(8,128)S(1)} collective-permute-done((f32[3,128,256]{2,1,0:T(8,128)}, f32[3,128,256]{2,1,0:T(8,128)S(1)}, u32[]{:S(2)}, u32[]{:S(2)}) %collective-permute-start.19) | collective-permute-done | bytes 393248 | tf_op jit(solution)/shard_map/ppermute | solution.py:351
  103.4 6.7 %collective-permute-done.20.refs_1_ = f32[3,128,256]{2,1,0:T(8,128)S(1)} collective-permute-done((f32[3,128,256]{2,1,0:T(8,128)S(1)}, f32[3,128,256]{2,1,0:T(8,128)S(1)}, u32[]{:S(2)}, u32[]{:S(2)}) %collective-permute-start.20) | collective-permute-done | bytes 393248 | tf_op jit(solution)/shard_map/ppermute | solution.py:351
  115.1 7.0 %collective-permute-done.21.refs_1_ = f32[3,128,256]{2,1,0:T(8,128)S(1)} collective-permute-done((f32[3,128,256]{2,1,0:T(8,128)S(1)}, f32[3,128,256]{2,1,0:T(8,128)S(1)}, u32[]{:S(2)}, u32[]{:S(2)}) %collective-permute-start.21) | collective-permute-done | bytes 393248 | tf_op jit(solution)/shard_map/ppermute | solution.py:351
  126.5 7.5 %collective-permute-done.22.refs_1_ = f32[3,128,256]{2,1,0:T(8,128)S(1)} collective-permute-done((f32[3,128,256]{2,1,0:T(8,128)S(1)}, f32[3,128,256]{2,1,0:T(8,128)S(1)}, u32[]{:S(2)}, u32[]{:S(2)}) %collective-permute-start.22) | collective-permute-done | bytes 393248 | tf_op jit(solution)/shard_map/ppermute | solution.py:351
  139.6 5.4 %order.1.plan_ref = s32[105]{0:T(128)} custom-call(s32[86]{0:T(128)} %cols_ref.3, s32[1,16]{1,0:T(1,128)} %counts_ref, s32[3]{0:T(128)} %copy-done.24), custom_call_target="tpu_custom_call" | custom-call | tf_op jit(solution)/shard_map/order/pallas_call | solution.py:218
  147.2 2.6 %copy-done.2 = f32[86,128,128]{2,1,0:T(8,128)S(1)} copy-done((f32[86,128,128]{2,1,0:T(8,128)S(1)}, f32[86,128,128]{2,1,0:T(8,128)}, u32[]{:S(2)}) %copy-start.2) | copy-done | bytes 5636120
  151.4 5.8 %add.38 = (f32[16,128,256]{2,1,0:T(8,128)S(1)}, f32[86,128,128]{2,1,0:T(8,128)S(1)}) custom-call(s32[105]{0:T(128)S(1)} %copy-done.23, f32[86,128,128]{2,1,0:T(8,128)S(1)} %copy-done.2, f32[16,128,256]{2,1,0:T(8,128)S(1)} %bitcast.10, f32[3,128,256]{2,1,0:T(8,128)S(1)} %copy-done.4), custom_call_target="tpu_custom_call" | custom-call | flops 167772160 | bytes 2097152 | tf_op jit(solution)/shard_map/add/pallas_call | solution.py:294
  157.2 2.9 %add.39.refs_3_ = f32[16,128,256]{2,1,0:T(8,128)S(1)} custom-call(s32[105]{0:T(128)S(1)} %copy-done.23, f32[86,128,128]{2,1,0:T(8,128)S(1)} %get-tuple-element.30.tiles_ref, f32[3,128,256]{2,1,0:T(8,128)} %collective-permute-done.17.refs_0_, f32[3,128,256]{2,1,0:T(8,128)} %collective-permute-done.25.refs_1_, ...), custom_call_target="tpu_custom_call", output_to_operand_aliasing={{}: (4, {})} | custom-call | flops 167772160 | bytes 2097152 | tf_op jit(solution)/shard_map/add/pallas_call | solution.py:294
  160.2 2.9 %add.40.refs_2_ = f32[16,128,256]{2,1,0:T(8,128)S(1)} custom-call(s32[105]{0:T(128)S(1)} %copy-done.23, f32[86,128,128]{2,1,0:T(8,128)S(1)} %get-tuple-element.30.tiles_ref, f32[8,128,256]{2,1,0:T(8,128)S(1)} %all-to-all-done.refs_1_.refs_0_, f32[3,128,256]{2,1,0:T(8,128)S(1)} %pick.3.refs_1_, ...), custom_call_target="tpu_custom_call", output_to_operand_aliasing={{}: (5, {})} | custom-call | flops 251658240 | bytes 2097152 | tf_op jit(solution)/shard_map/add/pallas_call | solution.py:294
  169.8 2.5 %add.44.refs_2_ = f32[16,128,256]{2,1,0:T(8,128)S(1)} custom-call(s32[105]{0:T(128)S(1)} %copy-done.23, f32[86,128,128]{2,1,0:T(8,128)S(1)} %get-tuple-element.30.tiles_ref, f32[3,128,256]{2,1,0:T(8,128)S(1)} %copy-done.20, f32[3,128,256]{2,1,0:T(8,128)S(1)} %copy-done.22, f32[16,128,256]{2,1,0:T(8,128)S(1)} %add.43.refs_2_), custom_call_target="tpu_custom_call", output_to_operand_aliasing={{}: (4, {})} | custom-call | flops 167772160 | bytes 2097152 | tf_op jit(solution)/shard_map/add/pallas_call | solution.py:294
  (111 shorter events, 64.7 us)
Async XLA Ops:
  8.0 5.7 %collective-permute-start.10 = (s32[8,8]{1,0:T(8,128)S(1)}, s32[8,8]{1,0:T(8,128)S(1)}, u32[]{:S(2)}, u32[]{:S(2)}) collective-permute-start(s32[8,8]{1,0:T(8,128)S(1)} %add.27.refs_1_), channel_id=1, source_target_pairs={{0,24},{4,28},{8,16},{12,20},{16,8},{20,12},{24,0},{28,4},{1,25},{... | collective-permute-start | bytes 776 | tf_op jit(solution)/shard_map/ppermute | solution.py:329
  20.7 61.4 %all-to-all-start = ((f32[8,128,256]{2,1,0:T(8,128)}), f32[8,128,256]{2,1,0:T(8,128)S(1)}, u32[]{:S(2)}, u32[]{:S(2)}) async-start(f32[8,128,256]{2,1,0:T(8,128)} %pick.2), calls=%async_computation | async-start | bytes 2097152 | tf_op jit(solution)/shard_map/all_to_all | solution.py:340
  26.4 8.8 %collective-permute-start = (f32[128,256]{1,0:T(8,128)S(1)}, f32[128,256]{1,0:T(8,128)S(1)}, u32[]{:S(2)}, u32[]{:S(2)}) collective-permute-start(f32[128,256]{1,0:T(8,128)S(1)} %get-tuple-element.21), channel_id=1, source_target_pairs={{0,4},{4,0},{8,12},{12,8},{16,20},{20,16},{24,28},{28,24},{1,5},{5... | collective-permute-start | bytes 393224 | tf_op jit(solution)/shard_map/ppermute | solution.py:327
  28.5 17.7 %collective-permute-start.1 = (f32[128,256]{1,0:T(8,128)S(1)}, f32[128,256]{1,0:T(8,128)S(1)}, u32[]{:S(2)}, u32[]{:S(2)}) collective-permute-start(f32[128,256]{1,0:T(8,128)S(1)} %get-tuple-element.22), channel_id=1, source_target_pairs={{0,8},{4,12},{8,0},{12,4},{16,24},{20,28},{24,16},{28,20},{1,9},{5... | collective-permute-start | bytes 393224 | tf_op jit(solution)/shard_map/ppermute | solution.py:327
  29.9 20.9 %collective-permute-start.2 = (f32[128,256]{1,0:T(8,128)S(1)}, f32[128,256]{1,0:T(8,128)S(1)}, u32[]{:S(2)}, u32[]{:S(2)}) collective-permute-start(f32[128,256]{1,0:T(8,128)S(1)} %get-tuple-element.23), channel_id=1, source_target_pairs={{0,12},{4,8},{8,4},{12,0},{16,28},{20,24},{24,20},{28,16},{1,13},{... | collective-permute-start | bytes 393224 | tf_op jit(solution)/shard_map/ppermute | solution.py:327
  30.0 34.8 %collective-permute-start.3 = (f32[128,256]{1,0:T(8,128)S(1)}, f32[128,256]{1,0:T(8,128)S(1)}, u32[]{:S(2)}, u32[]{:S(2)}) collective-permute-start(f32[128,256]{1,0:T(8,128)S(1)} %get-tuple-element.24), channel_id=1, source_target_pairs={{0,16},{4,20},{8,24},{12,28},{16,0},{20,4},{24,8},{28,12},{1,17},{... | collective-permute-start | bytes 393224 | tf_op jit(solution)/shard_map/ppermute | solution.py:327
  32.9 35.3 %collective-permute-start.4 = (f32[128,256]{1,0:T(8,128)S(1)}, f32[128,256]{1,0:T(8,128)S(1)}, u32[]{:S(2)}, u32[]{:S(2)}) collective-permute-start(f32[128,256]{1,0:T(8,128)S(1)} %get-tuple-element.25), channel_id=1, source_target_pairs={{0,20},{4,16},{8,28},{12,24},{16,4},{20,0},{24,12},{28,8},{1,21},{... | collective-permute-start | bytes 393224 | tf_op jit(solution)/shard_map/ppermute | solution.py:327
  35.2 33.0 %collective-permute-start.5 = (f32[128,256]{1,0:T(8,128)S(1)}, f32[128,256]{1,0:T(8,128)S(1)}, u32[]{:S(2)}, u32[]{:S(2)}) collective-permute-start(f32[128,256]{1,0:T(8,128)S(1)} %get-tuple-element.26), channel_id=1, source_target_pairs={{0,24},{4,28},{8,16},{12,20},{16,8},{20,12},{24,0},{28,4},{1,25},{... | collective-permute-start | bytes 393224 | tf_op jit(solution)/shard_map/ppermute | solution.py:327
  46.1 22.0 %collective-permute-start.6 = (f32[128,256]{1,0:T(8,128)S(1)}, f32[128,256]{1,0:T(8,128)S(1)}, u32[]{:S(2)}, u32[]{:S(2)}) collective-permute-start(f32[128,256]{1,0:T(8,128)S(1)} %get-tuple-element.27), channel_id=1, source_target_pairs={{0,28},{4,24},{8,20},{12,16},{16,12},{20,8},{24,4},{28,0},{1,29},{... | collective-permute-start | bytes 393224 | tf_op jit(solution)/shard_map/ppermute | solution.py:327
  69.4 10.1 %collective-permute-start.17 = (f32[3,128,256]{2,1,0:T(8,128)S(1)}, f32[3,128,256]{2,1,0:T(8,128)}, u32[]{:S(2)}, u32[]{:S(2)}) collective-permute-start(f32[3,128,256]{2,1,0:T(8,128)S(1)} %share.1.refs_1_), channel_id=1, source_target_pairs={{0,8},{8,16},{16,24},{24,28},{28,20},{20,12},{12,4},{4,0},{1,9},{9... | collective-permute-start | bytes 1179656 | tf_op jit(solution)/shard_map/ppermute | solution.py:351
  79.5 9.3 %collective-permute-start.18 = (f32[3,128,256]{2,1,0:T(8,128)}, f32[3,128,256]{2,1,0:T(8,128)}, u32[]{:S(2)}, u32[]{:S(2)}) collective-permute-start(f32[3,128,256]{2,1,0:T(8,128)} %collective-permute-done.17.refs_0_), channel_id=1, source_target_pairs={{0,8},{8,16},{16,24},{24,28},{28,20},{20,12},{12,4},{4,0},{1,9},{9... | collective-permute-start | bytes 1179656 | tf_op jit(solution)/shard_map/ppermute | solution.py:351
  83.2 8.8 %collective-permute-start.11 = (f32[3,128,256]{2,1,0:T(8,128)S(1)}, f32[3,128,256]{2,1,0:T(8,128)S(1)}, u32[]{:S(2)}, u32[]{:S(2)}) collective-permute-start(f32[3,128,256]{2,1,0:T(8,128)S(1)} %pick.3.refs_1_), channel_id=1, source_target_pairs={{8,0},{16,8},{24,16},{28,24},{20,28},{12,20},{4,12},{0,4},{9,1},{1... | collective-permute-start | bytes 1179656 | tf_op jit(solution)/shard_map/ppermute | solution.py:351
  88.8 10.2 %collective-permute-start.19 = (f32[3,128,256]{2,1,0:T(8,128)}, f32[3,128,256]{2,1,0:T(8,128)S(1)}, u32[]{:S(2)}, u32[]{:S(2)}) collective-permute-start(f32[3,128,256]{2,1,0:T(8,128)} %collective-permute-done.18.refs_2_), channel_id=1, source_target_pairs={{0,8},{8,16},{16,24},{24,28},{28,20},{20,12},{12,4},{4,0},{1,9},{9... | collective-permute-start | bytes 1179656 | tf_op jit(solution)/shard_map/ppermute | solution.py:351
  92.0 10.2 %collective-permute-start.12 = (f32[3,128,256]{2,1,0:T(8,128)S(1)}, f32[3,128,256]{2,1,0:T(8,128)S(1)}, u32[]{:S(2)}, u32[]{:S(2)}) collective-permute-start(f32[3,128,256]{2,1,0:T(8,128)S(1)} %collective-permute-done.11.refs_0_), channel_id=1, source_target_pairs={{8,0},{16,8},{24,16},{28,24},{20,28},{12,20},{4,12},{0,4},{9,1},{1... | collective-permute-start | bytes 1179656 | tf_op jit(solution)/shard_map/ppermute | solution.py:351
  99.1 11.1 %collective-permute-start.20 = (f32[3,128,256]{2,1,0:T(8,128)S(1)}, f32[3,128,256]{2,1,0:T(8,128)S(1)}, u32[]{:S(2)}, u32[]{:S(2)}) collective-permute-start(f32[3,128,256]{2,1,0:T(8,128)S(1)} %collective-permute-done.19.refs_1_), channel_id=1, source_target_pairs={{0,8},{8,16},{16,24},{24,28},{28,20},{20,12},{12,4},{4,0},{1,9},{9... | collective-permute-start | bytes 1179656 | tf_op jit(solution)/shard_map/ppermute | solution.py:351
  102.2 11.2 %collective-permute-start.13 = (f32[3,128,256]{2,1,0:T(8,128)S(1)}, f32[3,128,256]{2,1,0:T(8,128)S(1)}, u32[]{:S(2)}, u32[]{:S(2)}) collective-permute-start(f32[3,128,256]{2,1,0:T(8,128)S(1)} %collective-permute-done.12.refs_0_), channel_id=1, source_target_pairs={{8,0},{16,8},{24,16},{28,24},{20,28},{12,20},{4,12},{0,4},{9,1},{1... | collective-permute-start | bytes 1179656 | tf_op jit(solution)/shard_map/ppermute | solution.py:351
  110.1 12.0 %collective-permute-start.21 = (f32[3,128,256]{2,1,0:T(8,128)S(1)}, f32[3,128,256]{2,1,0:T(8,128)S(1)}, u32[]{:S(2)}, u32[]{:S(2)}) collective-permute-start(f32[3,128,256]{2,1,0:T(8,128)S(1)} %collective-permute-done.20.refs_1_), channel_id=1, source_target_pairs={{0,8},{8,16},{16,24},{24,28},{28,20},{20,12},{12,4},{4,0},{1,9},{9... | collective-permute-start | bytes 1179656 | tf_op jit(solution)/shard_map/ppermute | solution.py:351
  113.4 12.0 %collective-permute-start.14 = (f32[3,128,256]{2,1,0:T(8,128)S(1)}, f32[3,128,256]{2,1,0:T(8,128)S(1)}, u32[]{:S(2)}, u32[]{:S(2)}) collective-permute-start(f32[3,128,256]{2,1,0:T(8,128)S(1)} %collective-permute-done.13.refs_0_), channel_id=1, source_target_pairs={{8,0},{16,8},{24,16},{28,24},{20,28},{12,20},{4,12},{0,4},{9,1},{1... | collective-permute-start | bytes 1179656 | tf_op jit(solution)/shard_map/ppermute | solution.py:351
  122.1 11.9 %collective-permute-start.22 = (f32[3,128,256]{2,1,0:T(8,128)S(1)}, f32[3,128,256]{2,1,0:T(8,128)S(1)}, u32[]{:S(2)}, u32[]{:S(2)}) collective-permute-start(f32[3,128,256]{2,1,0:T(8,128)S(1)} %collective-permute-done.21.refs_1_), channel_id=1, source_target_pairs={{0,8},{8,16},{16,24},{24,28},{28,20},{20,12},{12,4},{4,0},{1,9},{9... | collective-permute-start | bytes 1179656 | tf_op jit(solution)/shard_map/ppermute | solution.py:351
  125.3 12.0 %collective-permute-start.15 = (f32[3,128,256]{2,1,0:T(8,128)S(1)}, f32[3,128,256]{2,1,0:T(8,128)S(1)}, u32[]{:S(2)}, u32[]{:S(2)}) collective-permute-start(f32[3,128,256]{2,1,0:T(8,128)S(1)} %collective-permute-done.14.refs_0_), channel_id=1, source_target_pairs={{8,0},{16,8},{24,16},{28,24},{20,28},{12,20},{4,12},{0,4},{9,1},{1... | collective-permute-start | bytes 1179656 | tf_op jit(solution)/shard_map/ppermute | solution.py:351
  134.7 10.3 %collective-permute-start.23 = (f32[3,128,256]{2,1,0:T(8,128)S(1)}, f32[3,128,256]{2,1,0:T(8,128)}, u32[]{:S(2)}, u32[]{:S(2)}) collective-permute-start(f32[3,128,256]{2,1,0:T(8,128)S(1)} %pick.3.refs_1_), channel_id=1, source_target_pairs={{0,8},{8,16},{16,24},{24,28},{28,20},{20,12},{12,4},{4,0},{1,9},{9... | collective-permute-start | bytes 1179656 | tf_op jit(solution)/shard_map/ppermute | solution.py:351
  137.2 20.0 %collective-permute-start.25 = (f32[3,128,256]{2,1,0:T(8,128)}, f32[3,128,256]{2,1,0:T(8,128)}, u32[]{:S(2)}, u32[]{:S(2)}) collective-permute-start(f32[3,128,256]{2,1,0:T(8,128)} %copy-done.3), channel_id=1, source_target_pairs={{8,0},{16,8},{24,16},{28,24},{20,28},{12,20},{4,12},{0,4},{9,1},{1... | collective-permute-start | bytes 1179656 | tf_op jit(solution)/shard_map/ppermute | solution.py:351
  138.8 36.0 %collective-permute-start.16 = (f32[2,128,256]{2,1,0:T(8,128)}, f32[2,128,256]{2,1,0:T(8,128)}, u32[]{:S(2)}, u32[]{:S(2)}) collective-permute-start(f32[2,128,256]{2,1,0:T(8,128)} %slice.8), channel_id=1, source_target_pairs={{8,0},{16,8},{24,16},{28,24},{20,28},{12,20},{4,12},{0,4},{9,1},{1... | collective-permute-start | bytes 786440 | tf_op jit(solution)/shard_map/ppermute | solution.py:351
  146.0 28.8 %collective-permute-start.24 = (f32[1,128,256]{2,1,0:T(8,128)S(1)}, f32[1,128,256]{2,1,0:T(8,128)S(1)}, u32[]{:S(2)}, u32[]{:S(2)}) collective-permute-start(f32[1,128,256]{2,1,0:T(8,128)S(1)} %slice.9), channel_id=1, source_target_pairs={{0,8},{8,16},{16,24},{24,28},{28,20},{20,12},{12,4},{4,0},{1,9},{9... | collective-permute-start | bytes 393224 | tf_op jit(solution)/shard_map/ppermute | solution.py:351
  (33 other events, 198.5 us)
